TPU v7x, 512 devices: a whole 4x4x16 slice. The times are simulated.
512 devices in a mesh: ctx: 64 (over z, y), head: 8 (over x, core).
Axes of the slice: x: 4, y: 4, z: 16, core: 2. Of those that a mesh axis runs over, the one named last changes fastest.
Arguments:
- tokens: bfloat16 [16384, 2048], P('ctx', 'head'), may hold values from -6 to 6
- qkv_weight: bfloat16 [2048, 3, 2048], P('ctx', None, 'head'), may hold values from -0.125 to 0.125
- out_gain: float32 [2048], P('head'), may hold values from 0.1 to 1.9
Outputs:
- attended: bfloat16 [16384, 2048], P('ctx', 'head')
All inputs are finite; a program needn't handle non-finite values.
Results may differ from a plain program's by a relative error of at most 0.001.
Values may be sent and summed in bfloat16 or wider, within the bound.
No kernel may reach another device: no remote copies, remote signals or barrier semaphores. Data moves between devices by JAX's collectives and lax.ppermute only.
A program may use at most 64 MiB of HBM per device.

v0:
```python
import functools

import jax
import jax.numpy as jnp
from jax import lax
from jax.experimental import pallas as pl
from jax.experimental.pallas import tpu as pltpu
from jax.sharding import Mesh, PartitionSpec as P


HD = 128
HALF = HD // 2
PACK = 72
ROWS = PACK + HD
PART = 104
epsilon = 1e-06
f32 = jnp.float32
bf16 = jnp.bfloat16
VM = pl.BlockSpec(memory_space=pltpu.VMEM)


def split(x):
    high = x.astype(bf16)
    return high, (x - high.astype(f32)).astype(bf16)


def mm2(a, b, ca, cb):
    dims = (((ca,), (cb,)), ((), ()))
    dot = lambda x, y: lax.dot_general(x, y, dims, preferred_element_type=f32)
    return dot(a[0], b[0]) + (dot(a[0], b[1]) + dot(a[1], b[0]))


def mm(a, b, ca=1, cb=0):
    return mm2(split(a), split(b), ca, cb)


def dot(x, y, ca=1, cb=0):
    return lax.dot_general(x, y, (((ca,), (cb,)), ((), ())), preferred_element_type=f32)


def left3(x):
    return jnp.concatenate([x[0], x[0], x[1]], axis=1)


def right3(y, axis):
    return jnp.concatenate([y[0], y[1], y[0]], axis=axis)


def narrow(x, y, cy=0):
    return dot(left3(x), right3(y, cy), 1, cy)


def wide(x, y):
    both = dot(x[0], jnp.concatenate([y[0], y[1]], axis=1))
    return both[:, :HD] + both[:, HD:] + dot(x[1], y[0])


def tril(x):
    n = x.shape[0]
    rows = lax.broadcasted_iota(jnp.int32, (n, n), 0)
    cols = lax.broadcasted_iota(jnp.int32, (n, n), 1)
    return jnp.where(rows >= cols, x, 0.0)


def corner_ids():
    rows = lax.broadcasted_iota(jnp.int32, (HALF, HALF), 0)
    return rows, lax.broadcasted_iota(jnp.int32, (HALF, HALF), 1)


def triu(x):
    n = x.shape[0]
    rows = lax.broadcasted_iota(jnp.int32, (n, n), 0)
    cols = lax.broadcasted_iota(jnp.int32, (n, n), 1)
    return jnp.where(rows <= cols, x, 0.0)


def pack_sym(s):
    rows, cols = corner_ids()
    a, b, d = s[:HALF, :HALF], s[:HALF, HALF:], s[HALF:, HALF:]
    diag = jnp.sum(jnp.where(rows == cols, d, 0.0), axis=0, keepdims=True)
    diag = jnp.broadcast_to(jnp.concatenate([diag, diag], axis=1), (PACK - HALF, HD))
    return jnp.concatenate([jnp.concatenate([b, jnp.where(rows <= cols, a, d)], axis=1), diag], axis=0)


def unpack_sym(p):
    rows, cols = corner_ids()
    b, tri = p[:HALF, :HALF], p[:HALF, HALF:]
    flip = tri.T
    a = jnp.where(rows <= cols, tri, flip)
    d = jnp.where(rows > cols, tri, flip)
    d = jnp.where(rows == cols, p[HALF : HALF + 1, :HALF], d)
    return jnp.concatenate(
        [jnp.concatenate([a, b], axis=1), jnp.concatenate([b.T, d], axis=1)], axis=0
    )


def place():
    y = lax.axis_index("y")
    return lax.rem(y, 2), lax.axis_index("core")


def ring():
    return lax.rem(lax.axis_index("z") + lax.axis_index("core"), 2)


def ring_groups(zs):
    return [[z * 2 + (z + g) % 2 for z in range(zs)] for g in range(2)]


def project_kernel(mine, tok, own, out_ref, wf):
    b, c = place()
    half = c if mine else 1 - c
    for z in range(own.shape[0]):
        zh, z1, z0 = z // 4, z // 2 % 2, z % 2
        for f in range(2):
            near = 32 * (b if f == 0 else 1 - b)
            at = pl.ds(pl.multiple_of(zh * 256 + z0 * 128 + 64 * z1 + near, 32), 32)
            for ch in range(3):
                wf[at, ch * HD : (ch + 1) * HD] = own[z, f, ch]
    for t in range(2):
        x = jnp.concatenate([tok[4 * f + 2 * half + t] for f in range(4)], axis=1)
        out_ref[256 * t : 256 * t + 256] = jnp.dot(x, wf[...], preferred_element_type=f32)


def moment_kernel(keep, got, q_ref, k_ref, v_ref, blk_ref, pay_ref):
    for t in range(2):
        rows = slice(t * 256, t * 256 + 256)
        proj = keep[rows] + got[rows]
        q, k, v = proj[:, :HD], proj[:, HD : 2 * HD], proj[:, 2 * HD :]
        q_ref[rows], k_ref[rows], v_ref[rows] = q, k, v
        q2, k2, v2 = split(q), split(k), split(v)
        w2 = split(wide(split(triu(narrow(k2, q2, 1))), v2))
        kh, kl = k2[0].T, k2[1].T
        a = dot(kh, jnp.concatenate([k2[0], k2[1], w2[0], w2[1]], axis=1))
        d = dot(kl, jnp.concatenate([k2[0], w2[0]], axis=1))
        s = a[:, :HD] + a[:, HD : 2 * HD] + d[:, :HD]
        m = a[:, 2 * HD : 3 * HD] + a[:, 3 * HD :] + d[:, HD:]
        cc = wide((q2[0].T, q2[1].T), v2)
        if t == 0:
            s_all, c_all, m_all = s, cc, m
            blk_ref[0], blk_ref[1], blk_ref[2] = s, cc, m
        else:
            m_all = m_all + m + narrow(split(s_all), split(cc))
            s_all, c_all = s_all + s, c_all + cc
    packed = pack_sym(s_all)
    for h in range(2):
        cols = slice(h * HALF, h * HALF + HALF)
        half = jnp.concatenate([c_all[:, cols], m_all[:, cols]], axis=1)
        for zb in range(2):
            slot = 2 * zb + (zb + h) % 2
            pay_ref[slot, :PACK] = packed
            pay_ref[slot, PACK:] = half


def local_kernel(q_ref, k_ref, v_ref, blk_ref, raw_ref):
    for t in range(2):
        rows = slice(t * 256, t * 256 + 256)
        q2 = split(q_ref[rows])
        low = split(tril(narrow(q2, split(k_ref[rows]), 1)))
        pair = mm2(low, low, 1, 1)
        if t == 1:
            qs = narrow(q2, split(blk_ref[0]))
            pair = pair + narrow(split(qs), q2, 1)
        raw = wide(split(tril(pair)), split(v_ref[rows]))
        if t == 1:
            raw = raw + narrow(q2, split(blk_ref[2]))
        raw_ref[rows] = raw


def pair_kernel(got, pay_ref, in_ref, s_in_ref, all_ref):
    _, c = place()
    zb = lax.rem(lax.axis_index("z"), 2)
    pos = 2 * zb + c
    s = jnp.zeros((PACK, HD), f32)
    cm = jnp.zeros((HD, HD), f32)
    s_in = s
    before = [cm, cm]
    left = lax.broadcasted_iota(jnp.int32, (HD, HD), 1) < HALF
    for i in range(4):
        s_in = jnp.where(pos == i, s, s_in)
        before[i % 2] = jnp.where(zb == i // 2, cm, before[i % 2])
        new = got[i, PACK:]
        if i:
            cross = mm(unpack_sym(s), new[:, :HALF])
            cross = jnp.concatenate([jnp.zeros_like(cross), cross], axis=1)
            cm = cm + new + cross
        else:
            cm = new
        s = s + got[i, :PACK]
    all_ref[:PACK] = s
    all_ref[PACK:ROWS] = cm
    all_ref[ROWS:] = jnp.zeros((2 * PART - ROWS, HD), f32)
    pay_ref[...] = all_ref[pl.ds(pl.multiple_of(zb * PART, 8), PART)]
    in_ref[0], in_ref[1] = before
    s_in_ref[...] = s_in


def prior_kernel(got, in_ref, s_in_ref, s_ref, keep_ref, send_ref):
    _, c = place()
    pair = lax.div(lax.axis_index("z"), 2)
    n = got.shape[0]
    s = jnp.zeros((PACK, HD), f32)
    m = jnp.zeros((HD, HALF), f32)
    lefts, rights = [], []
    for p in range(n - 1):
        live = p < pair
        if p:
            lefts.append(unpack_sym(s))
            rights.append(jnp.where(live, got[p, PACK:ROWS, :HALF], 0.0))
        m = m + jnp.where(live, got[p, PACK:ROWS, HALF:], 0.0)
        s = s + jnp.where(live, got[p, :PACK], 0.0)
    m = m + mm(jnp.concatenate(lefts, axis=1), jnp.concatenate(rights, axis=0))
    full = unpack_sym(s)
    both = jnp.concatenate([in_ref[0][:, :HALF], in_ref[1][:, :HALF]], axis=1)
    cross = mm(full, both)
    m0 = m + in_ref[0][:, HALF:] + cross[:, :HALF]
    m1 = m + in_ref[1][:, HALF:] + cross[:, HALF:]
    s_ref[...] = full + unpack_sym(s_in_ref[...])
    keep_ref[...] = jnp.where(c == 0, m0, m1)
    send_ref[...] = jnp.where(c == 0, m1, m0)


def cross_kernel(q_ref, v_ref, raw_ref, blk_ref, s_ref, out_ref):
    s2 = split(s_ref[...])
    for t in range(2):
        rows = slice(t * 256, t * 256 + 256)
        q2 = split(q_ref[rows])
        qs = split(narrow(q2, s2))
        scores = tril(narrow(qs, q2, 1))
        raw = raw_ref[rows] + wide(split(scores), split(v_ref[rows]))
        if t == 1:
            raw = raw + narrow(qs, split(blk_ref[1]))
        out_ref[rows] = raw


def final_kernel(q_ref, raw_ref, keep_ref, other_ref, gain_ref, gain_far_ref, near_ref, far_ref):
    b, c = place()
    h = ring()
    keep, other = keep_ref[...], other_ref[...]
    m2 = split(
        jnp.concatenate(
            [jnp.where(h == 0, keep, other), jnp.where(h == 0, other, keep)], axis=1
        )
    )
    y = lax.axis_index("y")
    gain = jnp.where(lax.div(y, 2) == c, gain_ref[...], gain_far_ref[...])
    gain = jnp.where(b == 0, gain[0:1], gain[1:2])
    for t in range(2):
        rows = slice(t * 256, t * 256 + 256)
        raw = raw_ref[rows] + narrow(split(q_ref[rows]), m2)
        mean_sq = jnp.mean(raw * raw, axis=-1, keepdims=True)
        out = (raw * lax.rsqrt(mean_sq + epsilon) * gain).astype(bf16)

        @pl.when(b == t)
        def _():
            near_ref[...] = out

        @pl.when(b != t)
        def _():
            far_ref[...] = out


def call(kernel, outs, flops, moved, scratch=()):
    return pl.pallas_call(
        kernel,
        out_shape=outs,
        scratch_shapes=list(scratch),
        compiler_params=pltpu.CompilerParams(vmem_limit_bytes=32 * 2**20),
        cost_estimate=pl.CostEstimate(flops=flops, bytes_accessed=moved, transcendentals=0),
    )


def pair_swap(flip):
    return [
        ((2 * a + b) * 2 + c, (2 * c + (b ^ flip)) * 2 + a)
        for a in range(2)
        for b in range(2)
        for c in range(2)
    ]


def weight_perm(zs, flip):
    pairs = []
    for z in range(zs):
        zh, z1, z0 = z // 4, z // 2 % 2, z % 2
        for y in range(4):
            a, b = y // 2, y % 2
            for c in range(2):
                to = (4 * zh + 2 * a + z0) * 8 + (2 * c + (b ^ flip)) * 2 + (z1 ^ z0)
                pairs.append((z * 8 + y * 2 + c, to))
    return pairs


def body(zs, tokens, weight, gain):
    shape = jax.ShapeDtypeStruct
    b = lax.rem(lax.axis_index("y"), 2)
    yc, zyc = ("y", "core"), ("z", "y", "core")
    core_swap = [(0, 1), (1, 0)]
    rows, mats = shape((512, HD), f32), lambda n: shape((n, HD, HD), f32)
    wide = shape((512, 3 * HD), f32)
    first, second = weight[:, :, :HD], weight[:, :, HD:]
    same = jnp.where(b == 0, first, second).transpose(1, 0, 2)
    flip = jnp.where(b == 0, second, first).transpose(1, 0, 2)
    same = lax.ppermute(same, zyc, weight_perm(zs, 0))
    flip = lax.ppermute(flip, zyc, weight_perm(zs, 1))
    turn = [(z * 2 + c, z * 2 + (c ^ z % 2)) for z in range(zs) for c in range(2)]
    tokens = lax.ppermute(tokens, ("z", "core"), turn)
    tok = lax.all_to_all(jnp.broadcast_to(tokens[None], (16,) + tokens.shape), ("x", "y"), 0, 0)
    own = lax.all_gather(
        jnp.stack([same, flip]), ("z", "core"), axis_index_groups=ring_groups(zs)
    )
    scratch = [pltpu.VMEM((zs * 64, 3 * HD), bf16)]
    send = call(functools.partial(project_kernel, False), wide, 400 * 10**6, 3 * 10**6, scratch)(tok, own)
    got = lax.ppermute(send, "core", core_swap)
    keep = call(functools.partial(project_kernel, True), wide, 400 * 10**6, 3 * 10**6, scratch)(tok, own)
    q, k, v, blk, pay = call(
        moment_kernel,
        (rows, rows, rows, mats(3), shape((4, ROWS, HD), f32)),
        600 * 10**6,
        3 * 10**6,
    )(keep, got)
    groups = [[(2 * p + i) * 2 + j for i in range(2) for j in range(2)] for p in range(zs // 2)]
    got = lax.all_to_all(pay, ("z", "core"), 0, 0, axis_index_groups=groups)
    gain, pay = lax.optimization_barrier((gain, pay))
    gain = gain.reshape(2, HD)
    gain_far = lax.ppermute(gain, "core", core_swap)
    raw = call(local_kernel, rows, 800 * 10**6, 2 * 10**6)(q, k, v, blk)
    total, inner, s_in = call(
        pair_kernel,
        (shape((PART, HD), f32), mats(2), shape((PACK, HD), f32)),
        10**8,
        10**6,
        [pltpu.VMEM((2 * PART, HD), f32)],
    )(got)
    totals = lax.all_gather(total, ("z", "core"), axis_index_groups=ring_groups(zs))
    totals = totals.reshape(zs // 2, 2 * PART, HD)
    s, keep, send = call(
        prior_kernel, (shape((HD, HD), f32), shape((HD, HALF), f32), shape((HD, HALF), f32)), 10**8, 10**6
    )(totals, inner, s_in)
    other_m = lax.ppermute(send, "core", core_swap)
    raw = call(cross_kernel, rows, 500 * 10**6, 2 * 10**6)(q, v, raw, blk, s)
    half = shape((256, HD), bf16)
    near, far = call(final_kernel, (half, half), 10**8, 10**6)(q, raw, keep, other_m, gain, gain_far)
    near = lax.ppermute(near, yc, pair_swap(0))
    far = lax.ppermute(far, yc, pair_swap(1))
    left = jnp.where(b == 0, near, far)
    right = jnp.where(b == 0, far, near)
    return jnp.concatenate([left, right], axis=1)


def solution(mesh):
    zs = mesh.shape["ctx"] // 4
    fine = Mesh(mesh.devices.reshape(zs, 4, 4, 2), ("z", "y", "x", "core"))
    ctx, head = ("z", "y"), ("x", "core")
    return jax.shard_map(
        functools.partial(body, zs),
        mesh=fine,
        in_specs=(P(ctx, head), P(ctx, None, head), P(head)),
        out_specs=P(ctx, head),
        check_vma=False,
    )
```

profile of v0, /device:TPU:7, one launch (start us, length us, event | category | flops | bytes accessed | tf_op | source)
XLA Modules:
  0.0 139.0 jit_solution(1496909958566104975)
XLA Ops:
  0.0 1.6 %collective-permute-start = (bf16[256,256]{1,0:T(8,128)(2,1)}, bf16[256,256]{1,0:T(8,128)(2,1)S(1)}, u32[]{:S(2)}, u32[]{:S(2)}) collective-permute-start(bf16[256,256]{1,0:T(8,128)(2,1)} %param.3), channel_id=1, source_target_pairs={{0,0},{1,1},{32,33},{33,32},{64,64},{65,65},{96,97},{97,96},{128,1... | collective-permute-start | bytes 393224 | tf_op jit(solution)/shard_map/ppermute | solution.py:307
  1.6 0.0 collective-permute-done
  1.6 1.5 %broadcast_in_dim.2 = bf16[16,256,256]{2,1,0:T(8,128)(2,1)} broadcast(bf16[256,256]{1,0:T(8,128)(2,1)S(1)} %collective-permute-done), dimensions={1,2} | broadcast | bytes 2228224 | tf_op jit(solution)/shard_map/broadcast_in_dim | solution.py:308
  3.1 0.0 copy-start.1
  3.1 7.0 %all-to-all-start = ((bf16[16,256,256]{2,1,0:T(8,128)(2,1)}), bf16[16,256,256]{2,1,0:T(8,128)(2,1)S(1)}, u32[]{:S(2)}, u32[]{:S(2)}) async-start(bf16[16,256,256]{2,1,0:T(8,128)(2,1)} %broadcast_in_dim.2), calls=%async_computation | async-start | bytes 4194304 | tf_op jit(solution)/shard_map/all_to_all | solution.py:308
  10.1 0.0 copy-done.1
  10.1 7.4 %collective-permute-start.2 = (bf16[3,32,128]{2,1,0:T(8,128)(2,1)S(1)}, bf16[3,32,128]{2,1,0:T(8,128)(2,1)S(1)}, u32[]{:S(2)}, u32[]{:S(2)}) collective-permute-start(bf16[3,32,128]{2,1,0:T(8,128)(2,1)S(1)} %get-tuple-element.36), channel_id=1, source_target_pairs={{0,8},{1,24},{8,0},{9,16},{16,72},{17,88},{24,64},{25,80},{32,41},... | collective-permute-start | bytes 73736 | tf_op jit(solution)/shard_map/ppermute | solution.py:305
  17.6 3.5 %collective-permute-start.1 = (bf16[3,32,128]{2,1,0:T(8,128)(2,1)S(1)}, bf16[3,32,128]{2,1,0:T(8,128)(2,1)S(1)}, u32[]{:S(2)}, u32[]{:S(2)}) collective-permute-start(bf16[3,32,128]{2,1,0:T(8,128)(2,1)S(1)} %get-tuple-element.35), channel_id=1, source_target_pairs={{0,0},{1,16},{8,8},{9,24},{16,64},{17,80},{24,72},{25,88},{32,33},... | collective-permute-start | bytes 73736 | tf_op jit(solution)/shard_map/ppermute | solution.py:304
  21.0 0.0 collective-permute-done.2
  21.0 11.5 %collective-permute-done.1 = bf16[3,32,128]{2,1,0:T(8,128)(2,1)S(1)} collective-permute-done((bf16[3,32,128]{2,1,0:T(8,128)(2,1)S(1)}, bf16[3,32,128]{2,1,0:T(8,128)(2,1)S(1)}, u32[]{:S(2)}, u32[]{:S(2)}) %collective-permute-start.1) | collective-permute-done | bytes 24608 | tf_op jit(solution)/shard_map/ppermute | solution.py:304
  32.6 41.6 %all-gather = bf16[32,3,32,128]{3,2,1,0:T(8,128)(2,1)S(1)} all-gather(bf16[2,3,32,128]{3,2,1,0:T(8,128)(2,1)S(1)} %pad_maximum_fusion.1), channel_id=2, replica_groups={{0,33,64,97,128,161,192,225,256,289,320,353,384,417,448,481},{1,32,65,9..., dimensions={0}, use_global_device_ids=true | all-gather | bytes 835584 | tf_op jit(solution)/shard_map/all_gather | solution.py:309
  74.2 0.0 all-to-all-done.tok
  74.2 0.8 shard_map.38
  75.0 3.3 %collective-permute-start.3 = (f32[512,384]{1,0:T(8,128)S(1)}, f32[512,384]{1,0:T(8,128)S(1)}, u32[]{:S(2)}, u32[]{:S(2)}) collective-permute-start(f32[512,384]{1,0:T(8,128)S(1)} %shard_map.38), channel_id=1, source_target_pairs={{0,1},{1,0},{2,3},{3,2},{4,5},{5,4},{6,7},{7,6},{8,9},{9,8},{10,11... | collective-permute-start | bytes 2359304 | tf_op jit(solution)/shard_map/ppermute | solution.py:314
  78.4 0.8 shard_map.37.keep
  79.2 0.0 copy-start
  79.2 1.0 collective-permute-done.3.got
  80.2 2.3 %shard_map.39 = (f32[512,128]{1,0:T(8,128)S(1)}, f32[512,128]{1,0:T(8,128)S(1)}, f32[512,128]{1,0:T(8,128)S(1)}, f32[3,128,128]{2,1,0:T(8,128)S(1)}, f32[4,200,128]{2,1,0:T(8,128)}) custom-call(f32[512,384]{1,0:T(8,128)S(1)} %shard_map.37.keep, f32[512,384]{1,0:T(8,128)S(1)} %collective-permute-done.3.got), custom_call_target="tpu_custom_call" | custom-call | flops 600000000 | bytes 3000000 | tf_op jit(solution)/shard_map/pallas_call | solution.py:316
  82.5 3.8 %all-to-all-start.1 = ((f32[4,200,128]{2,1,0:T(8,128)}), f32[4,200,128]{2,1,0:T(8,128)S(1)}, u32[]{:S(2)}, u32[]{:S(2)}) async-start(f32[4,200,128]{2,1,0:T(8,128)} %get-tuple-element.23), calls=%async_computation.1 | async-start | bytes 819200 | tf_op jit(solution)/shard_map/all_to_all | solution.py:323
  86.3 0.0 copy-done
  86.3 2.0 %collective-permute-start.5 = (f32[2,128]{1,0:T(2,128)S(1)}, f32[2,128]{1,0:T(2,128)S(1)}, u32[]{:S(2)}, u32[]{:S(2)}) collective-permute-start(f32[2,128]{1,0:T(2,128)S(1)} %bitcast.12), channel_id=1, source_target_pairs={{0,1},{1,0},{2,3},{3,2},{4,5},{5,4},{6,7},{7,6},{8,9},{9,8},{10,11... | collective-permute-start | bytes 3080 | tf_op jit(solution)/shard_map/ppermute | solution.py:326
  88.3 1.5 %shard_map.40.raw_ref = f32[512,128]{1,0:T(8,128)S(1)} custom-call(f32[512,128]{1,0:T(8,128)S(1)} %get-tuple-element.19.q_ref, f32[512,128]{1,0:T(8,128)S(1)} %get-tuple-element.21.k_ref, f32[512,128]{1,0:T(8,128)S(1)} %get-tuple-element.20.v_ref, f32[3,128,128]{2,1,0:T(8,128)S(1)} %get-tuple-element.22.blk_ref), custom_call_target="tpu_custom_call" | custom-call | flops 800000000 | bytes 2000000 | tf_op jit(solution)/shard_map/pallas_call | solution.py:327
  89.8 3.1 %all-to-all-done.1.got = f32[4,200,128]{2,1,0:T(8,128)S(1)} async-done(((f32[4,200,128]{2,1,0:T(8,128)}), f32[4,200,128]{2,1,0:T(8,128)S(1)}, u32[]{:S(2)}, u32[]{:S(2)}) %all-to-all-start.1) | async-done | bytes 409632 | tf_op jit(solution)/shard_map/all_to_all | solution.py:323
  93.0 0.5 shard_map.41
  93.5 29.2 %all-gather.1 = f32[1664,128]{1,0:T(8,128)S(1)} all-gather(f32[104,128]{1,0:T(8,128)S(1)} %get-tuple-element.24), channel_id=3, replica_groups={{0,33,64,97,128,161,192,225,256,289,320,353,384,417,448,481},{1,32,65,9..., dimensions={0}, use_global_device_ids=true | all-gather | bytes 905216 | tf_op jit(solution)/shard_map/all_gather | solution.py:335
  122.7 1.0 shard_map.42
  123.7 2.0 %collective-permute-start.4 = (f32[128,64]{1,0:T(8,128)S(1)}, f32[128,64]{1,0:T(8,128)S(1)}, u32[]{:S(2)}, u32[]{:S(2)}) collective-permute-start(f32[128,64]{1,0:T(8,128)S(1)} %get-tuple-element.29), channel_id=1, source_target_pairs={{0,1},{1,0},{2,3},{3,2},{4,5},{5,4},{6,7},{7,6},{8,9},{9,8},{10,11... | collective-permute-start | bytes 98312 | tf_op jit(solution)/shard_map/ppermute | solution.py:340
  125.7 1.1 shard_map.43.raw_ref
  126.8 0.0 collective-permute-done.5.gain_far_ref
  126.8 0.0 collective-permute-done.4.other_ref
  126.8 0.7 shard_map.44
  127.5 4.0 %collective-permute-start.6 = (bf16[256,128]{1,0:T(8,128)(2,1)S(1)}, bf16[256,128]{1,0:T(8,128)(2,1)S(1)}, u32[]{:S(2)}, u32[]{:S(2)}) collective-permute-start(bf16[256,128]{1,0:T(8,128)(2,1)S(1)} %get-tuple-element.31), channel_id=1, source_target_pairs={{0,0},{1,16},{8,8},{9,24},{16,1},{17,17},{24,9},{25,25},{2,2},{3,1... | collective-permute-start | bytes 196616 | tf_op jit(solution)/shard_map/ppermute | solution.py:344
  131.6 3.5 %collective-permute-start.7 = (bf16[256,128]{1,0:T(8,128)(2,1)S(1)}, bf16[256,128]{1,0:T(8,128)(2,1)S(1)}, u32[]{:S(2)}, u32[]{:S(2)}) collective-permute-start(bf16[256,128]{1,0:T(8,128)(2,1)S(1)} %get-tuple-element.32), channel_id=1, source_target_pairs={{0,8},{1,24},{8,0},{9,16},{16,9},{17,25},{24,1},{25,17},{2,10},{3,... | collective-permute-start | bytes 196616 | tf_op jit(solution)/shard_map/ppermute | solution.py:345
  135.1 0.0 collective-permute-done.6
  135.1 3.3 %collective-permute-done.7 = bf16[256,128]{1,0:T(8,128)(2,1)S(1)} collective-permute-done((bf16[256,128]{1,0:T(8,128)(2,1)S(1)}, bf16[256,128]{1,0:T(8,128)(2,1)S(1)}, u32[]{:S(2)}, u32[]{:S(2)}) %collective-permute-start.7) | collective-permute-done | bytes 65568 | tf_op jit(solution)/shard_map/ppermute | solution.py:345
  138.4 0.7 pad_maximum_fusion
  (3 shorter events, 0.0 us)
Async XLA Ops:
  0.0 1.6 %collective-permute-start = (bf16[256,256]{1,0:T(8,128)(2,1)}, bf16[256,256]{1,0:T(8,128)(2,1)S(1)}, u32[]{:S(2)}, u32[]{:S(2)}) collective-permute-start(bf16[256,256]{1,0:T(8,128)(2,1)} %param.3), channel_id=1, source_target_pairs={{0,0},{1,1},{32,33},{33,32},{64,64},{65,65},{96,97},{97,96},{128,1... | collective-permute-start | bytes 393224 | tf_op jit(solution)/shard_map/ppermute | solution.py:307
  3.1 7.0 %copy-start.1 = (bf16[32,3,256]{2,0,1:T(8,128)(2,1)S(1)}, bf16[32,3,256]{2,0,1:T(8,128)(2,1)}, u32[]{:S(2)}) copy-start(bf16[32,3,256]{2,0,1:T(8,128)(2,1)} %param.4) | copy-start | bytes 147460
  3.1 71.1 %all-to-all-start = ((bf16[16,256,256]{2,1,0:T(8,128)(2,1)}), bf16[16,256,256]{2,1,0:T(8,128)(2,1)S(1)}, u32[]{:S(2)}, u32[]{:S(2)}) async-start(bf16[16,256,256]{2,1,0:T(8,128)(2,1)} %broadcast_in_dim.2), calls=%async_computation | async-start | bytes 4194304 | tf_op jit(solution)/shard_map/all_to_all | solution.py:308
  10.1 10.9 %collective-permute-start.2 = (bf16[3,32,128]{2,1,0:T(8,128)(2,1)S(1)}, bf16[3,32,128]{2,1,0:T(8,128)(2,1)S(1)}, u32[]{:S(2)}, u32[]{:S(2)}) collective-permute-start(bf16[3,32,128]{2,1,0:T(8,128)(2,1)S(1)} %get-tuple-element.36), channel_id=1, source_target_pairs={{0,8},{1,24},{8,0},{9,16},{16,72},{17,88},{24,64},{25,80},{32,41},... | collective-permute-start | bytes 73736 | tf_op jit(solution)/shard_map/ppermute | solution.py:305
  17.6 15.0 %collective-permute-start.1 = (bf16[3,32,128]{2,1,0:T(8,128)(2,1)S(1)}, bf16[3,32,128]{2,1,0:T(8,128)(2,1)S(1)}, u32[]{:S(2)}, u32[]{:S(2)}) collective-permute-start(bf16[3,32,128]{2,1,0:T(8,128)(2,1)S(1)} %get-tuple-element.35), channel_id=1, source_target_pairs={{0,0},{1,16},{8,8},{9,24},{16,64},{17,80},{24,72},{25,88},{32,33},... | collective-permute-start | bytes 73736 | tf_op jit(solution)/shard_map/ppermute | solution.py:304
  75.0 5.2 %collective-permute-start.3 = (f32[512,384]{1,0:T(8,128)S(1)}, f32[512,384]{1,0:T(8,128)S(1)}, u32[]{:S(2)}, u32[]{:S(2)}) collective-permute-start(f32[512,384]{1,0:T(8,128)S(1)} %shard_map.38), channel_id=1, source_target_pairs={{0,1},{1,0},{2,3},{3,2},{4,5},{5,4},{6,7},{7,6},{8,9},{9,8},{10,11... | collective-permute-start | bytes 2359304 | tf_op jit(solution)/shard_map/ppermute | solution.py:314
  79.2 7.2 %copy-start = (f32[256]{0:T(256)S(1)}, f32[256]{0:T(256)}, u32[]{:S(2)}) copy-start(f32[256]{0:T(256)} %param.5) | copy-start | bytes 3076
  82.5 10.4 %all-to-all-start.1 = ((f32[4,200,128]{2,1,0:T(8,128)}), f32[4,200,128]{2,1,0:T(8,128)S(1)}, u32[]{:S(2)}, u32[]{:S(2)}) async-start(f32[4,200,128]{2,1,0:T(8,128)} %get-tuple-element.23), calls=%async_computation.1 | async-start | bytes 819200 | tf_op jit(solution)/shard_map/all_to_all | solution.py:323
  86.3 40.5 %collective-permute-start.5 = (f32[2,128]{1,0:T(2,128)S(1)}, f32[2,128]{1,0:T(2,128)S(1)}, u32[]{:S(2)}, u32[]{:S(2)}) collective-permute-start(f32[2,128]{1,0:T(2,128)S(1)} %bitcast.12), channel_id=1, source_target_pairs={{0,1},{1,0},{2,3},{3,2},{4,5},{5,4},{6,7},{7,6},{8,9},{9,8},{10,11... | collective-permute-start | bytes 3080 | tf_op jit(solution)/shard_map/ppermute | solution.py:326
  123.7 3.1 %collective-permute-start.4 = (f32[128,64]{1,0:T(8,128)S(1)}, f32[128,64]{1,0:T(8,128)S(1)}, u32[]{:S(2)}, u32[]{:S(2)}) collective-permute-start(f32[128,64]{1,0:T(8,128)S(1)} %get-tuple-element.29), channel_id=1, source_target_pairs={{0,1},{1,0},{2,3},{3,2},{4,5},{5,4},{6,7},{7,6},{8,9},{9,8},{10,11... | collective-permute-start | bytes 98312 | tf_op jit(solution)/shard_map/ppermute | solution.py:340
  127.5 7.5 %collective-permute-start.6 = (bf16[256,128]{1,0:T(8,128)(2,1)S(1)}, bf16[256,128]{1,0:T(8,128)(2,1)S(1)}, u32[]{:S(2)}, u32[]{:S(2)}) collective-permute-start(bf16[256,128]{1,0:T(8,128)(2,1)S(1)} %get-tuple-element.31), channel_id=1, source_target_pairs={{0,0},{1,16},{8,8},{9,24},{16,1},{17,17},{24,9},{25,25},{2,2},{3,1... | collective-permute-start | bytes 196616 | tf_op jit(solution)/shard_map/ppermute | solution.py:344
  131.6 6.8 %collective-permute-start.7 = (bf16[256,128]{1,0:T(8,128)(2,1)S(1)}, bf16[256,128]{1,0:T(8,128)(2,1)S(1)}, u32[]{:S(2)}, u32[]{:S(2)}) collective-permute-start(bf16[256,128]{1,0:T(8,128)(2,1)S(1)} %get-tuple-element.32), channel_id=1, source_target_pairs={{0,8},{1,24},{8,0},{9,16},{16,9},{17,25},{24,1},{25,17},{2,10},{3,... | collective-permute-start | bytes 196616 | tf_op jit(solution)/shard_map/ppermute | solution.py:345
where the time goes:
time: 140 us; the launch traced here: 139 us
  blocking collectives  70.8 us (51%)
  starting transfers between devices  38.1 us (27%)
  waiting for transfers between devices  19 us (14%)
  Pallas kernels  8.74 us (6%)
  local copies, waits for them, and re-layouts  1.56 us (1%)
    all_gather x1, blocking collectives, body(): lax.all_gather(jnp.stack([same, flip]), ('z', 'core'), axis_index_groups=...  41.6 us
    all_gather x1, blocking collectives, body(): lax.all_gather(total, ('z', 'core'), axis_index_groups=ring_groups(zs))  29.2 us
    ppermute x1, waiting for transfers between devices, body(): same = lax.ppermute(same, zyc, weight_perm(zs, 0))  11.5 us
    ppermute x1, starting transfers between devices, body(): flip = lax.ppermute(flip, zyc, weight_perm(zs, 1))  7.42 us
    all_to_all x1, starting transfers between devices, body(): lax.all_to_all(jnp.broadcast_to(tokens[None], (16,) + tokens.shape), ('x'...  7 us
    ppermute x1, starting transfers between devices, body(): near = lax.ppermute(near, yc, pair_swap(0))  4 us
    all_to_all x1, starting transfers between devices, body(): got = lax.all_to_all(pay, ('z', 'core'), 0, 0, axis_index_groups=groups)  3.8 us
    ppermute x1, starting transfers between devices, body(): far = lax.ppermute(far, yc, pair_swap(1))  3.5 us
  transfers between devices with their start and end apart: 10, of which 4 were waited for; matrix products, arithmetic and copies ran while one was open for 0% of the time, Pallas kernels for 4%

commit v1 on v0

--- a/solution.py
+++ b/solution.py
@@ -107,18 +107,29 @@
     return [[z * 2 + (z + g) % 2 for z in range(zs)] for g in range(2)]
 
 
+def halve_kernel(tok, keep_ref, send_ref):
+    h = ring()
+    left, right = tok[:, :HD], tok[:, HD:]
+    even = jnp.concatenate([left[:, :HALF], right[:, :HALF]], axis=1)
+    odd = jnp.concatenate([left[:, HALF:], right[:, HALF:]], axis=1)
+    keep_ref[...] = jnp.where(h == 0, even, odd)
+    send_ref[...] = jnp.where(h == 0, odd, even)
+
+
 def project_kernel(mine, tok, own, out_ref, wf):
     b, c = place()
     half = c if mine else 1 - c
     for z in range(own.shape[0]):
         zh, z1, z0 = z // 4, z // 2 % 2, z % 2
+        side = 128 * (c if z1 == 0 else 1 - c)
         for f in range(2):
             near = 32 * (b if f == 0 else 1 - b)
-            at = pl.ds(pl.multiple_of(zh * 256 + z0 * 128 + 64 * z1 + near, 32), 32)
+            at = pl.ds(pl.multiple_of(zh * 256 + 64 * z0 + side + near, 32), 32)
             for ch in range(3):
                 wf[at, ch * HD : (ch + 1) * HD] = own[z, f, ch]
     for t in range(2):
-        x = jnp.concatenate([tok[4 * f + 2 * half + t] for f in range(4)], axis=1)
+        pieces = [(4 * f + 2 * half + t, side) for f in range(4) for side in range(2)]
+        x = jnp.concatenate([tok[slot, side] for slot, side in pieces], axis=1)
         out_ref[256 * t : 256 * t + 256] = jnp.dot(x, wf[...], preferred_element_type=f32)
 
 
@@ -280,15 +291,13 @@
 
 
 def weight_perm(zs, flip):
-    pairs = []
-    for z in range(zs):
-        zh, z1, z0 = z // 4, z // 2 % 2, z % 2
-        for y in range(4):
-            a, b = y // 2, y % 2
-            for c in range(2):
-                to = (4 * zh + 2 * a + z0) * 8 + (2 * c + (b ^ flip)) * 2 + (z1 ^ z0)
-                pairs.append((z * 8 + y * 2 + c, to))
-    return pairs
+    return [
+        (z * 8 + (2 * a + b) * 2 + c, z * 8 + (2 * c + (b ^ flip)) * 2 + (a ^ z % 2))
+        for z in range(zs)
+        for a in range(2)
+        for b in range(2)
+        for c in range(2)
+    ]
 
 
 def body(zs, tokens, weight, gain):
@@ -303,9 +312,12 @@
     flip = jnp.where(b == 0, second, first).transpose(1, 0, 2)
     same = lax.ppermute(same, zyc, weight_perm(zs, 0))
     flip = lax.ppermute(flip, zyc, weight_perm(zs, 1))
-    turn = [(z * 2 + c, z * 2 + (c ^ z % 2)) for z in range(zs) for c in range(2)]
-    tokens = lax.ppermute(tokens, ("z", "core"), turn)
-    tok = lax.all_to_all(jnp.broadcast_to(tokens[None], (16,) + tokens.shape), ("x", "y"), 0, 0)
+    part = shape((256, HD), bf16)
+    keep, send = call(halve_kernel, (part, part), 10**5, 3 * 10**5)(tokens)
+    got = lax.ppermute(send, "core", core_swap)
+    tok = jnp.stack([keep, got])
+    tok = jnp.broadcast_to(tok[None], (16,) + tok.shape)
+    tok = lax.all_to_all(tok, ("x", "y"), 0, 0)
     own = lax.all_gather(
         jnp.stack([same, flip]), ("z", "core"), axis_index_groups=ring_groups(zs)
     )

time: 140 us -> 141 us (level)
  blocking collectives: 70.8 us -> 64.5 us
  waiting for transfers between devices: 19 us -> 24.4 us
    ppermute x1, waiting for transfers between devices: 0.01 us -> 16.3 us  [body(): flip = lax.ppermute(flip, zyc, weight_perm(zs, 1))]
    ppermute x1, waiting for transfers between devices: 11.5 us -> 1.1 us  [body(): same = lax.ppermute(same, zyc, weight_perm(zs, 0))]
    all_gather x1, blocking collectives: 41.6 us -> 35.1 us  [body(): lax.all_gather(jnp.stack([same, flip]), ('z', 'core'), axis_index_groups=...]
    ppermute x1 -> x2, starting transfers between devices: 3.35 us -> 7.38 us  [body(): got = lax.ppermute(send, 'core', core_swap)]
    ppermute x1, starting transfers between devices: 7.42 us -> 4.84 us  [body(): flip = lax.ppermute(flip, zyc, weight_perm(zs, 1))]
    all_to_all x1, starting transfers between devices: 7 us -> 9.26 us  [body(): tok = lax.all_to_all(tok, ('x', 'y'), 0, 0)]
    ppermute x1, starting transfers between devices: 4 us -> 1.92 us  [body(): near = lax.ppermute(near, yc, pair_swap(0))]
    ppermute x1, starting transfers between devices: 3.5 us -> 5.31 us  [body(): far = lax.ppermute(far, yc, pair_swap(1))]
  transfers between devices with their start and end apart: 10 -> 10, of which waited for: 4 -> 6; matrix products, arithmetic and copies ran while one was open for 0% -> 0% of each run, Pallas kernels for 4% -> 4%
where the time goes in v1:
time: 141 us; the launch traced here: 140 us
  blocking collectives  64.5 us (46%)
  starting transfers between devices  38.7 us (27%)
  waiting for transfers between devices  24.4 us (17%)
  Pallas kernels  8.87 us (6%)
  local copies, waits for them, and re-layouts  2.72 us (2%)
    all_gather x1, blocking collectives, body(): lax.all_gather(jnp.stack([same, flip]), ('z', 'core'), axis_index_groups=...  35.1 us
    all_gather x1, blocking collectives, body(): lax.all_gather(total, ('z', 'core'), axis_index_groups=ring_groups(zs))  29.5 us
    ppermute x1, waiting for transfers between devices, body(): flip = lax.ppermute(flip, zyc, weight_perm(zs, 1))  16.3 us
    all_to_all x1, starting transfers between devices, body(): tok = lax.all_to_all(tok, ('x', 'y'), 0, 0)  9.26 us
    ppermute x2, starting transfers between devices, body(): got = lax.ppermute(send, 'core', core_swap)  7.38 us
    ppermute x1, starting transfers between devices, body(): far = lax.ppermute(far, yc, pair_swap(1))  5.31 us
    ppermute x1, starting transfers between devices, body(): flip = lax.ppermute(flip, zyc, weight_perm(zs, 1))  4.84 us
    all_to_all x1, starting transfers between devices, body(): got = lax.all_to_all(pay, ('z', 'core'), 0, 0, axis_index_groups=groups)  3.8 us
  transfers between devices with their start and end apart: 10, of which 6 were waited for; matrix products, arithmetic and copies ran while one was open for 0% of the time, Pallas kernels for 4%

profile of v1, /device:TPU:7, one launch (start us, length us, event | category | flops | bytes accessed | tf_op | source)
XLA Modules:
  0.0 140.1 jit_solution(7338935895152022063)
XLA Ops:
  0.0 0.0 copy-start
  0.0 0.9 copy-done
  0.9 0.1 shard_map.37
  1.0 2.6 %collective-permute-start = (bf16[256,128]{1,0:T(8,128)(2,1)S(1)}, bf16[256,128]{1,0:T(8,128)(2,1)S(1)}, u32[]{:S(2)}, u32[]{:S(2)}) collective-permute-start(bf16[256,128]{1,0:T(8,128)(2,1)S(1)} %get-tuple-element.22), channel_id=1, source_target_pairs={{0,1},{1,0},{2,3},{3,2},{4,5},{5,4},{6,7},{7,6},{8,9},{9,8},{10,11... | collective-permute-start | bytes 196616 | tf_op jit(solution)/shard_map/ppermute | solution.py:317
  3.6 0.9 collective-permute-done
  4.5 1.8 %broadcast_in_dim.2 = bf16[16,2,256,128]{3,2,1,0:T(8,128)(2,1)} broadcast(bf16[2,256,128]{2,1,0:T(8,128)(2,1)S(1)} %pad_maximum_fusion), dimensions={1,2,3} | broadcast | bytes 2228224 | tf_op jit(solution)/shard_map/broadcast_in_dim | solution.py:319
  6.3 0.0 copy-start.2
  6.3 9.3 %all-to-all-start = ((bf16[16,2,256,128]{3,2,1,0:T(8,128)(2,1)}), bf16[16,2,256,128]{3,2,1,0:T(8,128)(2,1)S(1)}, u32[]{:S(2)}, u32[]{:S(2)}) async-start(bf16[16,2,256,128]{3,2,1,0:T(8,128)(2,1)} %broadcast_in_dim.2), calls=%async_computation | async-start | bytes 4194304 | tf_op jit(solution)/shard_map/all_to_all | solution.py:320
  15.6 0.0 copy-done.2
  15.6 4.8 %collective-permute-start.2 = (bf16[3,32,128]{2,1,0:T(8,128)(2,1)S(1)}, bf16[3,32,128]{2,1,0:T(8,128)(2,1)S(1)}, u32[]{:S(2)}, u32[]{:S(2)}) collective-permute-start(bf16[3,32,128]{2,1,0:T(8,128)(2,1)S(1)} %get-tuple-element.40), channel_id=1, source_target_pairs={{0,8},{1,24},{8,0},{9,16},{16,9},{17,25},{24,1},{25,17},{32,41},{3... | collective-permute-start | bytes 73736 | tf_op jit(solution)/shard_map/ppermute | solution.py:314
  20.4 2.2 %collective-permute-start.1 = (bf16[3,32,128]{2,1,0:T(8,128)(2,1)S(1)}, bf16[3,32,128]{2,1,0:T(8,128)(2,1)S(1)}, u32[]{:S(2)}, u32[]{:S(2)}) collective-permute-start(bf16[3,32,128]{2,1,0:T(8,128)(2,1)S(1)} %get-tuple-element.39), channel_id=1, source_target_pairs={{0,0},{1,16},{8,8},{9,24},{16,1},{17,17},{24,9},{25,25},{32,33},{3... | collective-permute-start | bytes 73736 | tf_op jit(solution)/shard_map/ppermute | solution.py:313
  22.7 16.3 %collective-permute-done.2 = bf16[3,32,128]{2,1,0:T(8,128)(2,1)S(1)} collective-permute-done((bf16[3,32,128]{2,1,0:T(8,128)(2,1)S(1)}, bf16[3,32,128]{2,1,0:T(8,128)(2,1)S(1)}, u32[]{:S(2)}, u32[]{:S(2)}) %collective-permute-start.2) | collective-permute-done | bytes 24608 | tf_op jit(solution)/shard_map/ppermute | solution.py:314
  39.0 1.1 collective-permute-done.1
  40.1 35.1 %all-gather = bf16[32,3,32,128]{3,2,1,0:T(8,128)(2,1)S(1)} all-gather(bf16[2,3,32,128]{3,2,1,0:T(8,128)(2,1)S(1)} %pad_maximum_fusion.2), channel_id=2, replica_groups={{0,33,64,97,128,161,192,225,256,289,320,353,384,417,448,481},{1,32,65,9..., dimensions={0}, use_global_device_ids=true | all-gather | bytes 835584 | tf_op jit(solution)/shard_map/all_gather | solution.py:321
  75.2 0.0 all-to-all-done.tok
  75.2 0.8 shard_map.39
  76.0 4.8 %collective-permute-start.3 = (f32[512,384]{1,0:T(8,128)S(1)}, f32[512,384]{1,0:T(8,128)S(1)}, u32[]{:S(2)}, u32[]{:S(2)}) collective-permute-start(f32[512,384]{1,0:T(8,128)S(1)} %shard_map.39), channel_id=1, source_target_pairs={{0,1},{1,0},{2,3},{3,2},{4,5},{5,4},{6,7},{7,6},{8,9},{9,8},{10,11... | collective-permute-start | bytes 2359304 | tf_op jit(solution)/shard_map/ppermute | solution.py:326
  80.8 0.8 shard_map.38.keep
  81.7 0.0 copy-start.1
  81.7 1.0 collective-permute-done.3.got
  82.7 2.3 %shard_map.40 = (f32[512,128]{1,0:T(8,128)S(1)}, f32[512,128]{1,0:T(8,128)S(1)}, f32[512,128]{1,0:T(8,128)S(1)}, f32[3,128,128]{2,1,0:T(8,128)S(1)}, f32[4,200,128]{2,1,0:T(8,128)}) custom-call(f32[512,384]{1,0:T(8,128)S(1)} %shard_map.38.keep, f32[512,384]{1,0:T(8,128)S(1)} %collective-permute-done.3.got), custom_call_target="tpu_custom_call" | custom-call | flops 600000000 | bytes 3000000 | tf_op jit(solution)/shard_map/pallas_call | solution.py:328
  85.0 3.8 %all-to-all-start.1 = ((f32[4,200,128]{2,1,0:T(8,128)}), f32[4,200,128]{2,1,0:T(8,128)S(1)}, u32[]{:S(2)}, u32[]{:S(2)}) async-start(f32[4,200,128]{2,1,0:T(8,128)} %get-tuple-element.27), calls=%async_computation.1 | async-start | bytes 819200 | tf_op jit(solution)/shard_map/all_to_all | solution.py:335
  88.8 0.0 copy-done.1
  88.8 2.0 %collective-permute-start.5 = (f32[2,128]{1,0:T(2,128)S(1)}, f32[2,128]{1,0:T(2,128)S(1)}, u32[]{:S(2)}, u32[]{:S(2)}) collective-permute-start(f32[2,128]{1,0:T(2,128)S(1)} %bitcast.15), channel_id=1, source_target_pairs={{0,1},{1,0},{2,3},{3,2},{4,5},{5,4},{6,7},{7,6},{8,9},{9,8},{10,11... | collective-permute-start | bytes 3080 | tf_op jit(solution)/shard_map/ppermute | solution.py:338
  90.8 1.5 %shard_map.41.raw_ref = f32[512,128]{1,0:T(8,128)S(1)} custom-call(f32[512,128]{1,0:T(8,128)S(1)} %get-tuple-element.23.q_ref, f32[512,128]{1,0:T(8,128)S(1)} %get-tuple-element.25.k_ref, f32[512,128]{1,0:T(8,128)S(1)} %get-tuple-element.24.v_ref, f32[3,128,128]{2,1,0:T(8,128)S(1)} %get-tuple-element.26.blk_ref), custom_call_target="tpu_custom_call" | custom-call | flops 800000000 | bytes 2000000 | tf_op jit(solution)/shard_map/pallas_call | solution.py:339
  92.3 3.1 %all-to-all-done.1.got = f32[4,200,128]{2,1,0:T(8,128)S(1)} async-done(((f32[4,200,128]{2,1,0:T(8,128)}), f32[4,200,128]{2,1,0:T(8,128)S(1)}, u32[]{:S(2)}, u32[]{:S(2)}) %all-to-all-start.1) | async-done | bytes 409632 | tf_op jit(solution)/shard_map/all_to_all | solution.py:335
  95.5 0.5 shard_map.42
  96.0 29.5 %all-gather.1 = f32[1664,128]{1,0:T(8,128)S(1)} all-gather(f32[104,128]{1,0:T(8,128)S(1)} %get-tuple-element.28), channel_id=3, replica_groups={{0,33,64,97,128,161,192,225,256,289,320,353,384,417,448,481},{1,32,65,9..., dimensions={0}, use_global_device_ids=true | all-gather | bytes 905216 | tf_op jit(solution)/shard_map/all_gather | solution.py:347
  125.4 1.0 shard_map.43
  126.4 2.0 %collective-permute-start.4 = (f32[128,64]{1,0:T(8,128)S(1)}, f32[128,64]{1,0:T(8,128)S(1)}, u32[]{:S(2)}, u32[]{:S(2)}) collective-permute-start(f32[128,64]{1,0:T(8,128)S(1)} %get-tuple-element.33), channel_id=1, source_target_pairs={{0,1},{1,0},{2,3},{3,2},{4,5},{5,4},{6,7},{7,6},{8,9},{9,8},{10,11... | collective-permute-start | bytes 98312 | tf_op jit(solution)/shard_map/ppermute | solution.py:352
  128.4 1.1 shard_map.44.raw_ref
  129.5 0.0 collective-permute-done.5.gain_far_ref
  129.6 0.0 collective-permute-done.4.other_ref
  129.6 0.7 shard_map.45
  130.3 1.9 %collective-permute-start.6 = (bf16[256,128]{1,0:T(8,128)(2,1)S(1)}, bf16[256,128]{1,0:T(8,128)(2,1)S(1)}, u32[]{:S(2)}, u32[]{:S(2)}) collective-permute-start(bf16[256,128]{1,0:T(8,128)(2,1)S(1)} %get-tuple-element.35), channel_id=1, source_target_pairs={{0,0},{1,16},{8,8},{9,24},{16,1},{17,17},{24,9},{25,25},{2,2},{3,1... | collective-permute-start | bytes 196616 | tf_op jit(solution)/shard_map/ppermute | solution.py:356
  132.2 5.3 %collective-permute-start.7 = (bf16[256,128]{1,0:T(8,128)(2,1)S(1)}, bf16[256,128]{1,0:T(8,128)(2,1)S(1)}, u32[]{:S(2)}, u32[]{:S(2)}) collective-permute-start(bf16[256,128]{1,0:T(8,128)(2,1)S(1)} %get-tuple-element.36), channel_id=1, source_target_pairs={{0,8},{1,24},{8,0},{9,16},{16,9},{17,25},{24,1},{25,17},{2,10},{3,... | collective-permute-start | bytes 196616 | tf_op jit(solution)/shard_map/ppermute | solution.py:357
  137.5 0.0 collective-permute-done.6
  137.5 1.9 %collective-permute-done.7 = bf16[256,128]{1,0:T(8,128)(2,1)S(1)} collective-permute-done((bf16[256,128]{1,0:T(8,128)(2,1)S(1)}, bf16[256,128]{1,0:T(8,128)(2,1)S(1)}, u32[]{:S(2)}, u32[]{:S(2)}) %collective-permute-start.7) | collective-permute-done | bytes 65568 | tf_op jit(solution)/shard_map/ppermute | solution.py:357
  139.5 0.7 pad_maximum_fusion.1
  (4 shorter events, 0.0 us)
Async XLA Ops:
  0.0 0.9 copy-start
  1.0 3.5 %collective-permute-start = (bf16[256,128]{1,0:T(8,128)(2,1)S(1)}, bf16[256,128]{1,0:T(8,128)(2,1)S(1)}, u32[]{:S(2)}, u32[]{:S(2)}) collective-permute-start(bf16[256,128]{1,0:T(8,128)(2,1)S(1)} %get-tuple-element.22), channel_id=1, source_target_pairs={{0,1},{1,0},{2,3},{3,2},{4,5},{5,4},{6,7},{7,6},{8,9},{9,8},{10,11... | collective-permute-start | bytes 196616 | tf_op jit(solution)/shard_map/ppermute | solution.py:317
  6.3 9.3 %copy-start.2 = (bf16[32,3,256]{2,0,1:T(8,128)(2,1)S(1)}, bf16[32,3,256]{2,0,1:T(8,128)(2,1)}, u32[]{:S(2)}) copy-start(bf16[32,3,256]{2,0,1:T(8,128)(2,1)} %param.4) | copy-start | bytes 147460
  6.3 68.9 %all-to-all-start = ((bf16[16,2,256,128]{3,2,1,0:T(8,128)(2,1)}), bf16[16,2,256,128]{3,2,1,0:T(8,128)(2,1)S(1)}, u32[]{:S(2)}, u32[]{:S(2)}) async-start(bf16[16,2,256,128]{3,2,1,0:T(8,128)(2,1)} %broadcast_in_dim.2), calls=%async_computation | async-start | bytes 4194304 | tf_op jit(solution)/shard_map/all_to_all | solution.py:320
  15.6 23.4 %collective-permute-start.2 = (bf16[3,32,128]{2,1,0:T(8,128)(2,1)S(1)}, bf16[3,32,128]{2,1,0:T(8,128)(2,1)S(1)}, u32[]{:S(2)}, u32[]{:S(2)}) collective-permute-start(bf16[3,32,128]{2,1,0:T(8,128)(2,1)S(1)} %get-tuple-element.40), channel_id=1, source_target_pairs={{0,8},{1,24},{8,0},{9,16},{16,9},{17,25},{24,1},{25,17},{32,41},{3... | collective-permute-start | bytes 73736 | tf_op jit(solution)/shard_map/ppermute | solution.py:314
  20.4 19.6 %collective-permute-start.1 = (bf16[3,32,128]{2,1,0:T(8,128)(2,1)S(1)}, bf16[3,32,128]{2,1,0:T(8,128)(2,1)S(1)}, u32[]{:S(2)}, u32[]{:S(2)}) collective-permute-start(bf16[3,32,128]{2,1,0:T(8,128)(2,1)S(1)} %get-tuple-element.39), channel_id=1, source_target_pairs={{0,0},{1,16},{8,8},{9,24},{16,1},{17,17},{24,9},{25,25},{32,33},{3... | collective-permute-start | bytes 73736 | tf_op jit(solution)/shard_map/ppermute | solution.py:313
  76.0 6.7 %collective-permute-start.3 = (f32[512,384]{1,0:T(8,128)S(1)}, f32[512,384]{1,0:T(8,128)S(1)}, u32[]{:S(2)}, u32[]{:S(2)}) collective-permute-start(f32[512,384]{1,0:T(8,128)S(1)} %shard_map.39), channel_id=1, source_target_pairs={{0,1},{1,0},{2,3},{3,2},{4,5},{5,4},{6,7},{7,6},{8,9},{9,8},{10,11... | collective-permute-start | bytes 2359304 | tf_op jit(solution)/shard_map/ppermute | solution.py:326
  81.7 7.1 %copy-start.1 = (f32[256]{0:T(256)S(1)}, f32[256]{0:T(256)}, u32[]{:S(2)}) copy-start(f32[256]{0:T(256)} %param.5) | copy-start | bytes 3076
  85.0 10.4 %all-to-all-start.1 = ((f32[4,200,128]{2,1,0:T(8,128)}), f32[4,200,128]{2,1,0:T(8,128)S(1)}, u32[]{:S(2)}, u32[]{:S(2)}) async-start(f32[4,200,128]{2,1,0:T(8,128)} %get-tuple-element.27), calls=%async_computation.1 | async-start | bytes 819200 | tf_op jit(solution)/shard_map/all_to_all | solution.py:335
  88.8 40.7 %collective-permute-start.5 = (f32[2,128]{1,0:T(2,128)S(1)}, f32[2,128]{1,0:T(2,128)S(1)}, u32[]{:S(2)}, u32[]{:S(2)}) collective-permute-start(f32[2,128]{1,0:T(2,128)S(1)} %bitcast.15), channel_id=1, source_target_pairs={{0,1},{1,0},{2,3},{3,2},{4,5},{5,4},{6,7},{7,6},{8,9},{9,8},{10,11... | collective-permute-start | bytes 3080 | tf_op jit(solution)/shard_map/ppermute | solution.py:338
  126.4 3.1 %collective-permute-start.4 = (f32[128,64]{1,0:T(8,128)S(1)}, f32[128,64]{1,0:T(8,128)S(1)}, u32[]{:S(2)}, u32[]{:S(2)}) collective-permute-start(f32[128,64]{1,0:T(8,128)S(1)} %get-tuple-element.33), channel_id=1, source_target_pairs={{0,1},{1,0},{2,3},{3,2},{4,5},{5,4},{6,7},{7,6},{8,9},{9,8},{10,11... | collective-permute-start | bytes 98312 | tf_op jit(solution)/shard_map/ppermute | solution.py:352
  130.3 7.2 %collective-permute-start.6 = (bf16[256,128]{1,0:T(8,128)(2,1)S(1)}, bf16[256,128]{1,0:T(8,128)(2,1)S(1)}, u32[]{:S(2)}, u32[]{:S(2)}) collective-permute-start(bf16[256,128]{1,0:T(8,128)(2,1)S(1)} %get-tuple-element.35), channel_id=1, source_target_pairs={{0,0},{1,16},{8,8},{9,24},{16,1},{17,17},{24,9},{25,25},{2,2},{3,1... | collective-permute-start | bytes 196616 | tf_op jit(solution)/shard_map/ppermute | solution.py:356
  132.2 7.2 %collective-permute-start.7 = (bf16[256,128]{1,0:T(8,128)(2,1)S(1)}, bf16[256,128]{1,0:T(8,128)(2,1)S(1)}, u32[]{:S(2)}, u32[]{:S(2)}) collective-permute-start(bf16[256,128]{1,0:T(8,128)(2,1)S(1)} %get-tuple-element.36), channel_id=1, source_target_pairs={{0,8},{1,24},{8,0},{9,16},{16,9},{17,25},{24,1},{25,17},{2,10},{3,... | collective-permute-start | bytes 196616 | tf_op jit(solution)/shard_map/ppermute | solution.py:357

commit v2 on v1

--- a/solution.py
+++ b/solution.py
@@ -133,34 +133,52 @@
         out_ref[256 * t : 256 * t + 256] = jnp.dot(x, wf[...], preferred_element_type=f32)
 
 
-def moment_kernel(keep, got, q_ref, k_ref, v_ref, blk_ref, pay_ref):
+def moment_kernel(keep, got, q_ref, k_ref, v_ref, blk_ref, pay_ref, stage, sems):
+    parts, sums = [], []
     for t in range(2):
         rows = slice(t * 256, t * 256 + 256)
         proj = keep[rows] + got[rows]
         q, k, v = proj[:, :HD], proj[:, HD : 2 * HD], proj[:, 2 * HD :]
         q_ref[rows], k_ref[rows], v_ref[rows] = q, k, v
         q2, k2, v2 = split(q), split(k), split(v)
+        turned = (k2[0].T, k2[1].T)
+        both = dot(turned[0], jnp.concatenate([k2[0], k2[1]], axis=1))
+        s = both[:, :HD] + (both[:, HD:] + both[:, HD:].T)
+        if t == 0:
+            blk_ref[0] = s
+        sums.append(s)
+        parts.append((q2, k2, v2, turned))
+    s_first = sums[0]
+    packed = pack_sym(sums[0] + sums[1])
+    stage[0, :PACK] = packed
+    head = slice(0, PACK)
+    copies = [
+        pltpu.make_async_copy(stage.at[0, head], pay_ref.at[slot, head], sems.at[0, slot])
+        for slot in range(4)
+    ]
+    for copy in copies:
+        copy.start()
+    for t, (q2, k2, v2, turned) in enumerate(parts):
         w2 = split(wide(split(triu(narrow(k2, q2, 1))), v2))
-        kh, kl = k2[0].T, k2[1].T
-        a = dot(kh, jnp.concatenate([k2[0], k2[1], w2[0], w2[1]], axis=1))
-        d = dot(kl, jnp.concatenate([k2[0], w2[0]], axis=1))
-        s = a[:, :HD] + a[:, HD : 2 * HD] + d[:, :HD]
-        m = a[:, 2 * HD : 3 * HD] + a[:, 3 * HD :] + d[:, HD:]
+        m = wide(turned, w2)
         cc = wide((q2[0].T, q2[1].T), v2)
         if t == 0:
-            s_all, c_all, m_all = s, cc, m
-            blk_ref[0], blk_ref[1], blk_ref[2] = s, cc, m
+            c_all, m_all = cc, m
+            blk_ref[1], blk_ref[2] = cc, m
         else:
-            m_all = m_all + m + narrow(split(s_all), split(cc))
-            s_all, c_all = s_all + s, c_all + cc
-    packed = pack_sym(s_all)
+            m_all = m_all + m + narrow(split(s_first), split(cc))
+            c_all = c_all + cc
+    tail = slice(PACK, ROWS)
     for h in range(2):
         cols = slice(h * HALF, h * HALF + HALF)
-        half = jnp.concatenate([c_all[:, cols], m_all[:, cols]], axis=1)
+        stage[h, PACK:] = jnp.concatenate([c_all[:, cols], m_all[:, cols]], axis=1)
         for zb in range(2):
             slot = 2 * zb + (zb + h) % 2
-            pay_ref[slot, :PACK] = packed
-            pay_ref[slot, PACK:] = half
+            copy = pltpu.make_async_copy(stage.at[h, tail], pay_ref.at[slot, tail], sems.at[1, slot])
+            copy.start()
+            copies.append(copy)
+    for copy in copies:
+        copy.wait()
 
 
 def local_kernel(q_ref, k_ref, v_ref, blk_ref, raw_ref):
@@ -271,9 +289,10 @@
             far_ref[...] = out
 
 
-def call(kernel, outs, flops, moved, scratch=()):
+def call(kernel, outs, flops, moved, scratch=(), **specs):
     return pl.pallas_call(
         kernel,
+        **specs,
         out_shape=outs,
         scratch_shapes=list(scratch),
         compiler_params=pltpu.CompilerParams(vmem_limit_bytes=32 * 2**20),
@@ -330,6 +349,8 @@
         (rows, rows, rows, mats(3), shape((4, ROWS, HD), f32)),
         600 * 10**6,
         3 * 10**6,
+        [pltpu.VMEM((2, ROWS, HD), f32), pltpu.SemaphoreType.DMA((2, 4))],
+        out_specs=(VM, VM, VM, VM, pl.BlockSpec(memory_space=pltpu.HBM)),
     )(keep, got)
     groups = [[(2 * p + i) * 2 + j for i in range(2) for j in range(2)] for p in range(zs // 2)]
     got = lax.all_to_all(pay, ("z", "core"), 0, 0, axis_index_groups=groups)

time: 141 us -> 141 us (level)
  no operation moved by 1% of the time
where the time goes in v2:
time: 141 us; the launch traced here: 140 us
  blocking collectives  64.5 us (46%)
  starting transfers between devices  38.7 us (27%)
  waiting for transfers between devices  24.4 us (17%)
  Pallas kernels  8.94 us (6%)
  local copies, waits for them, and re-layouts  2.72 us (2%)
    all_gather x1, blocking collectives, body(): lax.all_gather(jnp.stack([same, flip]), ('z', 'core'), axis_index_groups=...  35.1 us
    all_gather x1, blocking collectives, body(): lax.all_gather(total, ('z', 'core'), axis_index_groups=ring_groups(zs))  29.5 us
    ppermute x1, waiting for transfers between devices, body(): flip = lax.ppermute(flip, zyc, weight_perm(zs, 1))  16.3 us
    all_to_all x1, starting transfers between devices, body(): tok = lax.all_to_all(tok, ('x', 'y'), 0, 0)  9.26 us
    ppermute x2, starting transfers between devices, body(): got = lax.ppermute(send, 'core', core_swap)  7.38 us
    ppermute x1, starting transfers between devices, body(): far = lax.ppermute(far, yc, pair_swap(1))  5.31 us
    ppermute x1, starting transfers between devices, body(): flip = lax.ppermute(flip, zyc, weight_perm(zs, 1))  4.84 us
    all_to_all x1, starting transfers between devices, body(): got = lax.all_to_all(pay, ('z', 'core'), 0, 0, axis_index_groups=groups)  3.81 us
  transfers between devices with their start and end apart: 10, of which 6 were waited for; matrix products, arithmetic and copies ran while one was open for 0% of the time, Pallas kernels for 4%

profile of v2, /device:TPU:7, one launch (start us, length us, event | category | flops | bytes accessed | tf_op | source)
XLA Modules:
  0.0 140.2 jit_solution(5033191436481666438)
XLA Ops:
  0.0 0.0 copy-start
  0.0 0.9 copy-done
  0.9 0.1 shard_map.37
  1.0 2.6 %collective-permute-start = (bf16[256,128]{1,0:T(8,128)(2,1)S(1)}, bf16[256,128]{1,0:T(8,128)(2,1)S(1)}, u32[]{:S(2)}, u32[]{:S(2)}) collective-permute-start(bf16[256,128]{1,0:T(8,128)(2,1)S(1)} %get-tuple-element.22), channel_id=1, source_target_pairs={{0,1},{1,0},{2,3},{3,2},{4,5},{5,4},{6,7},{7,6},{8,9},{9,8},{10,11... | collective-permute-start | bytes 196616 | tf_op jit(solution)/shard_map/ppermute | solution.py:336
  3.6 0.9 collective-permute-done
  4.5 1.8 %broadcast_in_dim.2 = bf16[16,2,256,128]{3,2,1,0:T(8,128)(2,1)} broadcast(bf16[2,256,128]{2,1,0:T(8,128)(2,1)S(1)} %pad_maximum_fusion), dimensions={1,2,3} | broadcast | bytes 2228224 | tf_op jit(solution)/shard_map/broadcast_in_dim | solution.py:338
  6.3 0.0 copy-start.2
  6.3 9.3 %all-to-all-start = ((bf16[16,2,256,128]{3,2,1,0:T(8,128)(2,1)}), bf16[16,2,256,128]{3,2,1,0:T(8,128)(2,1)S(1)}, u32[]{:S(2)}, u32[]{:S(2)}) async-start(bf16[16,2,256,128]{3,2,1,0:T(8,128)(2,1)} %broadcast_in_dim.2), calls=%async_computation | async-start | bytes 4194304 | tf_op jit(solution)/shard_map/all_to_all | solution.py:339
  15.6 0.0 copy-done.2
  15.6 4.8 %collective-permute-start.2 = (bf16[3,32,128]{2,1,0:T(8,128)(2,1)S(1)}, bf16[3,32,128]{2,1,0:T(8,128)(2,1)S(1)}, u32[]{:S(2)}, u32[]{:S(2)}) collective-permute-start(bf16[3,32,128]{2,1,0:T(8,128)(2,1)S(1)} %get-tuple-element.40), channel_id=1, source_target_pairs={{0,8},{1,24},{8,0},{9,16},{16,9},{17,25},{24,1},{25,17},{32,41},{3... | collective-permute-start | bytes 73736 | tf_op jit(solution)/shard_map/ppermute | solution.py:333
  20.4 2.2 %collective-permute-start.1 = (bf16[3,32,128]{2,1,0:T(8,128)(2,1)S(1)}, bf16[3,32,128]{2,1,0:T(8,128)(2,1)S(1)}, u32[]{:S(2)}, u32[]{:S(2)}) collective-permute-start(bf16[3,32,128]{2,1,0:T(8,128)(2,1)S(1)} %get-tuple-element.39), channel_id=1, source_target_pairs={{0,0},{1,16},{8,8},{9,24},{16,1},{17,17},{24,9},{25,25},{32,33},{3... | collective-permute-start | bytes 73736 | tf_op jit(solution)/shard_map/ppermute | solution.py:332
  22.7 16.3 %collective-permute-done.2 = bf16[3,32,128]{2,1,0:T(8,128)(2,1)S(1)} collective-permute-done((bf16[3,32,128]{2,1,0:T(8,128)(2,1)S(1)}, bf16[3,32,128]{2,1,0:T(8,128)(2,1)S(1)}, u32[]{:S(2)}, u32[]{:S(2)}) %collective-permute-start.2) | collective-permute-done | bytes 24608 | tf_op jit(solution)/shard_map/ppermute | solution.py:333
  39.0 1.1 collective-permute-done.1
  40.1 35.1 %all-gather = bf16[32,3,32,128]{3,2,1,0:T(8,128)(2,1)S(1)} all-gather(bf16[2,3,32,128]{3,2,1,0:T(8,128)(2,1)S(1)} %pad_maximum_fusion.2), channel_id=2, replica_groups={{0,33,64,97,128,161,192,225,256,289,320,353,384,417,448,481},{1,32,65,9..., dimensions={0}, use_global_device_ids=true | all-gather | bytes 835584 | tf_op jit(solution)/shard_map/all_gather | solution.py:340
  75.2 0.0 all-to-all-done.tok
  75.2 0.8 shard_map.39
  76.0 4.8 %collective-permute-start.3 = (f32[512,384]{1,0:T(8,128)S(1)}, f32[512,384]{1,0:T(8,128)S(1)}, u32[]{:S(2)}, u32[]{:S(2)}) collective-permute-start(f32[512,384]{1,0:T(8,128)S(1)} %shard_map.39), channel_id=1, source_target_pairs={{0,1},{1,0},{2,3},{3,2},{4,5},{5,4},{6,7},{7,6},{8,9},{9,8},{10,11... | collective-permute-start | bytes 2359304 | tf_op jit(solution)/shard_map/ppermute | solution.py:345
  80.8 0.8 shard_map.38.keep
  81.7 0.0 copy-start.1
  81.7 1.0 collective-permute-done.3.got
  82.7 2.4 %shard_map.40 = (f32[512,128]{1,0:T(8,128)S(1)}, f32[512,128]{1,0:T(8,128)S(1)}, f32[512,128]{1,0:T(8,128)S(1)}, f32[3,128,128]{2,1,0:T(8,128)S(1)}, f32[4,200,128]{2,1,0:T(8,128)}) custom-call(f32[512,384]{1,0:T(8,128)S(1)} %shard_map.38.keep, f32[512,384]{1,0:T(8,128)S(1)} %collective-permute-done.3.got), custom_call_target="tpu_custom_call" | custom-call | flops 600000000 | bytes 3000000 | tf_op jit(solution)/shard_map/pallas_call | solution.py:347
  85.1 3.8 %all-to-all-start.1 = ((f32[4,200,128]{2,1,0:T(8,128)}), f32[4,200,128]{2,1,0:T(8,128)S(1)}, u32[]{:S(2)}, u32[]{:S(2)}) async-start(f32[4,200,128]{2,1,0:T(8,128)} %get-tuple-element.27), calls=%async_computation.1 | async-start | bytes 819200 | tf_op jit(solution)/shard_map/all_to_all | solution.py:356
  88.9 0.0 copy-done.1
  88.9 2.0 %collective-permute-start.5 = (f32[2,128]{1,0:T(2,128)S(1)}, f32[2,128]{1,0:T(2,128)S(1)}, u32[]{:S(2)}, u32[]{:S(2)}) collective-permute-start(f32[2,128]{1,0:T(2,128)S(1)} %bitcast.15), channel_id=1, source_target_pairs={{0,1},{1,0},{2,3},{3,2},{4,5},{5,4},{6,7},{7,6},{8,9},{9,8},{10,11... | collective-permute-start | bytes 3080 | tf_op jit(solution)/shard_map/ppermute | solution.py:359
  90.9 1.5 %shard_map.41.raw_ref = f32[512,128]{1,0:T(8,128)S(1)} custom-call(f32[512,128]{1,0:T(8,128)S(1)} %get-tuple-element.23.q_ref, f32[512,128]{1,0:T(8,128)S(1)} %get-tuple-element.25.k_ref, f32[512,128]{1,0:T(8,128)S(1)} %get-tuple-element.24.v_ref, f32[3,128,128]{2,1,0:T(8,128)S(1)} %get-tuple-element.26.blk_ref), custom_call_target="tpu_custom_call" | custom-call | flops 800000000 | bytes 2000000 | tf_op jit(solution)/shard_map/pallas_call | solution.py:360
  92.4 3.1 %all-to-all-done.1.got = f32[4,200,128]{2,1,0:T(8,128)S(1)} async-done(((f32[4,200,128]{2,1,0:T(8,128)}), f32[4,200,128]{2,1,0:T(8,128)S(1)}, u32[]{:S(2)}, u32[]{:S(2)}) %all-to-all-start.1) | async-done | bytes 409632 | tf_op jit(solution)/shard_map/all_to_all | solution.py:356
  95.5 0.5 shard_map.42
  96.1 29.5 %all-gather.1 = f32[1664,128]{1,0:T(8,128)S(1)} all-gather(f32[104,128]{1,0:T(8,128)S(1)} %get-tuple-element.28), channel_id=3, replica_groups={{0,33,64,97,128,161,192,225,256,289,320,353,384,417,448,481},{1,32,65,9..., dimensions={0}, use_global_device_ids=true | all-gather | bytes 905216 | tf_op jit(solution)/shard_map/all_gather | solution.py:368
  125.5 1.0 shard_map.43
  126.5 2.0 %collective-permute-start.4 = (f32[128,64]{1,0:T(8,128)S(1)}, f32[128,64]{1,0:T(8,128)S(1)}, u32[]{:S(2)}, u32[]{:S(2)}) collective-permute-start(f32[128,64]{1,0:T(8,128)S(1)} %get-tuple-element.33), channel_id=1, source_target_pairs={{0,1},{1,0},{2,3},{3,2},{4,5},{5,4},{6,7},{7,6},{8,9},{9,8},{10,11... | collective-permute-start | bytes 98312 | tf_op jit(solution)/shard_map/ppermute | solution.py:373
  128.5 1.1 shard_map.44.raw_ref
  129.6 0.0 collective-permute-done.5.gain_far_ref
  129.6 0.0 collective-permute-done.4.other_ref
  129.6 0.7 shard_map.45
  130.3 1.9 %collective-permute-start.6 = (bf16[256,128]{1,0:T(8,128)(2,1)S(1)}, bf16[256,128]{1,0:T(8,128)(2,1)S(1)}, u32[]{:S(2)}, u32[]{:S(2)}) collective-permute-start(bf16[256,128]{1,0:T(8,128)(2,1)S(1)} %get-tuple-element.35), channel_id=1, source_target_pairs={{0,0},{1,16},{8,8},{9,24},{16,1},{17,17},{24,9},{25,25},{2,2},{3,1... | collective-permute-start | bytes 196616 | tf_op jit(solution)/shard_map/ppermute | solution.py:377
  132.3 5.3 %collective-permute-start.7 = (bf16[256,128]{1,0:T(8,128)(2,1)S(1)}, bf16[256,128]{1,0:T(8,128)(2,1)S(1)}, u32[]{:S(2)}, u32[]{:S(2)}) collective-permute-start(bf16[256,128]{1,0:T(8,128)(2,1)S(1)} %get-tuple-element.36), channel_id=1, source_target_pairs={{0,8},{1,24},{8,0},{9,16},{16,9},{17,25},{24,1},{25,17},{2,10},{3,... | collective-permute-start | bytes 196616 | tf_op jit(solution)/shard_map/ppermute | solution.py:378
  137.6 0.0 collective-permute-done.6
  137.6 1.9 %collective-permute-done.7 = bf16[256,128]{1,0:T(8,128)(2,1)S(1)} collective-permute-done((bf16[256,128]{1,0:T(8,128)(2,1)S(1)}, bf16[256,128]{1,0:T(8,128)(2,1)S(1)}, u32[]{:S(2)}, u32[]{:S(2)}) %collective-permute-start.7) | collective-permute-done | bytes 65568 | tf_op jit(solution)/shard_map/ppermute | solution.py:378
  139.6 0.7 pad_maximum_fusion.1
  (4 shorter events, 0.0 us)
Async XLA Ops:
  0.0 0.9 copy-start
  1.0 3.5 %collective-permute-start = (bf16[256,128]{1,0:T(8,128)(2,1)S(1)}, bf16[256,128]{1,0:T(8,128)(2,1)S(1)}, u32[]{:S(2)}, u32[]{:S(2)}) collective-permute-start(bf16[256,128]{1,0:T(8,128)(2,1)S(1)} %get-tuple-element.22), channel_id=1, source_target_pairs={{0,1},{1,0},{2,3},{3,2},{4,5},{5,4},{6,7},{7,6},{8,9},{9,8},{10,11... | collective-permute-start | bytes 196616 | tf_op jit(solution)/shard_map/ppermute | solution.py:336
  6.3 9.3 %copy-start.2 = (bf16[32,3,256]{2,0,1:T(8,128)(2,1)S(1)}, bf16[32,3,256]{2,0,1:T(8,128)(2,1)}, u32[]{:S(2)}) copy-start(bf16[32,3,256]{2,0,1:T(8,128)(2,1)} %param.4) | copy-start | bytes 147460
  6.3 68.9 %all-to-all-start = ((bf16[16,2,256,128]{3,2,1,0:T(8,128)(2,1)}), bf16[16,2,256,128]{3,2,1,0:T(8,128)(2,1)S(1)}, u32[]{:S(2)}, u32[]{:S(2)}) async-start(bf16[16,2,256,128]{3,2,1,0:T(8,128)(2,1)} %broadcast_in_dim.2), calls=%async_computation | async-start | bytes 4194304 | tf_op jit(solution)/shard_map/all_to_all | solution.py:339
  15.6 23.4 %collective-permute-start.2 = (bf16[3,32,128]{2,1,0:T(8,128)(2,1)S(1)}, bf16[3,32,128]{2,1,0:T(8,128)(2,1)S(1)}, u32[]{:S(2)}, u32[]{:S(2)}) collective-permute-start(bf16[3,32,128]{2,1,0:T(8,128)(2,1)S(1)} %get-tuple-element.40), channel_id=1, source_target_pairs={{0,8},{1,24},{8,0},{9,16},{16,9},{17,25},{24,1},{25,17},{32,41},{3... | collective-permute-start | bytes 73736 | tf_op jit(solution)/shard_map/ppermute | solution.py:333
  20.4 19.6 %collective-permute-start.1 = (bf16[3,32,128]{2,1,0:T(8,128)(2,1)S(1)}, bf16[3,32,128]{2,1,0:T(8,128)(2,1)S(1)}, u32[]{:S(2)}, u32[]{:S(2)}) collective-permute-start(bf16[3,32,128]{2,1,0:T(8,128)(2,1)S(1)} %get-tuple-element.39), channel_id=1, source_target_pairs={{0,0},{1,16},{8,8},{9,24},{16,1},{17,17},{24,9},{25,25},{32,33},{3... | collective-permute-start | bytes 73736 | tf_op jit(solution)/shard_map/ppermute | solution.py:332
  76.0 6.7 %collective-permute-start.3 = (f32[512,384]{1,0:T(8,128)S(1)}, f32[512,384]{1,0:T(8,128)S(1)}, u32[]{:S(2)}, u32[]{:S(2)}) collective-permute-start(f32[512,384]{1,0:T(8,128)S(1)} %shard_map.39), channel_id=1, source_target_pairs={{0,1},{1,0},{2,3},{3,2},{4,5},{5,4},{6,7},{7,6},{8,9},{9,8},{10,11... | collective-permute-start | bytes 2359304 | tf_op jit(solution)/shard_map/ppermute | solution.py:345
  81.7 7.2 %copy-start.1 = (f32[256]{0:T(256)S(1)}, f32[256]{0:T(256)}, u32[]{:S(2)}) copy-start(f32[256]{0:T(256)} %param.5) | copy-start | bytes 3076
  85.1 10.4 %all-to-all-start.1 = ((f32[4,200,128]{2,1,0:T(8,128)}), f32[4,200,128]{2,1,0:T(8,128)S(1)}, u32[]{:S(2)}, u32[]{:S(2)}) async-start(f32[4,200,128]{2,1,0:T(8,128)} %get-tuple-element.27), calls=%async_computation.1 | async-start | bytes 819200 | tf_op jit(solution)/shard_map/all_to_all | solution.py:356
  88.9 40.7 %collective-permute-start.5 = (f32[2,128]{1,0:T(2,128)S(1)}, f32[2,128]{1,0:T(2,128)S(1)}, u32[]{:S(2)}, u32[]{:S(2)}) collective-permute-start(f32[2,128]{1,0:T(2,128)S(1)} %bitcast.15), channel_id=1, source_target_pairs={{0,1},{1,0},{2,3},{3,2},{4,5},{5,4},{6,7},{7,6},{8,9},{9,8},{10,11... | collective-permute-start | bytes 3080 | tf_op jit(solution)/shard_map/ppermute | solution.py:359
  126.5 3.1 %collective-permute-start.4 = (f32[128,64]{1,0:T(8,128)S(1)}, f32[128,64]{1,0:T(8,128)S(1)}, u32[]{:S(2)}, u32[]{:S(2)}) collective-permute-start(f32[128,64]{1,0:T(8,128)S(1)} %get-tuple-element.33), channel_id=1, source_target_pairs={{0,1},{1,0},{2,3},{3,2},{4,5},{5,4},{6,7},{7,6},{8,9},{9,8},{10,11... | collective-permute-start | bytes 98312 | tf_op jit(solution)/shard_map/ppermute | solution.py:373
  130.3 7.3 %collective-permute-start.6 = (bf16[256,128]{1,0:T(8,128)(2,1)S(1)}, bf16[256,128]{1,0:T(8,128)(2,1)S(1)}, u32[]{:S(2)}, u32[]{:S(2)}) collective-permute-start(bf16[256,128]{1,0:T(8,128)(2,1)S(1)} %get-tuple-element.35), channel_id=1, source_target_pairs={{0,0},{1,16},{8,8},{9,24},{16,1},{17,17},{24,9},{25,25},{2,2},{3,1... | collective-permute-start | bytes 196616 | tf_op jit(solution)/shard_map/ppermute | solution.py:377
  132.3 7.3 %collective-permute-start.7 = (bf16[256,128]{1,0:T(8,128)(2,1)S(1)}, bf16[256,128]{1,0:T(8,128)(2,1)S(1)}, u32[]{:S(2)}, u32[]{:S(2)}) collective-permute-start(bf16[256,128]{1,0:T(8,128)(2,1)S(1)} %get-tuple-element.36), channel_id=1, source_target_pairs={{0,8},{1,24},{8,0},{9,16},{16,9},{17,25},{24,1},{25,17},{2,10},{3,... | collective-permute-start | bytes 196616 | tf_op jit(solution)/shard_map/ppermute | solution.py:378

commit v3 on v1

--- a/solution.py
+++ b/solution.py
@@ -143,9 +143,9 @@
         w2 = split(wide(split(triu(narrow(k2, q2, 1))), v2))
         kh, kl = k2[0].T, k2[1].T
         a = dot(kh, jnp.concatenate([k2[0], k2[1], w2[0], w2[1]], axis=1))
-        d = dot(kl, jnp.concatenate([k2[0], w2[0]], axis=1))
-        s = a[:, :HD] + a[:, HD : 2 * HD] + d[:, :HD]
-        m = a[:, 2 * HD : 3 * HD] + a[:, 3 * HD :] + d[:, HD:]
+        cross = a[:, HD : 2 * HD]
+        s = a[:, :HD] + (cross + cross.T)
+        m = a[:, 2 * HD : 3 * HD] + a[:, 3 * HD :] + dot(kl, w2[0])
         cc = wide((q2[0].T, q2[1].T), v2)
         if t == 0:
             s_all, c_all, m_all = s, cc, m

time: 141 us -> 141 us (level)
  no operation moved by 1% of the time
where the time goes in v3:
time: 141 us; the launch traced here: 140 us
  blocking collectives  64.5 us (46%)
  starting transfers between devices  38.7 us (27%)
  waiting for transfers between devices  24.4 us (17%)
  Pallas kernels  8.87 us (6%)
  local copies, waits for them, and re-layouts  2.72 us (2%)
    all_gather x1, blocking collectives, body(): lax.all_gather(jnp.stack([same, flip]), ('z', 'core'), axis_index_groups=...  35.1 us
    all_gather x1, blocking collectives, body(): lax.all_gather(total, ('z', 'core'), axis_index_groups=ring_groups(zs))  29.5 us
    ppermute x1, waiting for transfers between devices, body(): flip = lax.ppermute(flip, zyc, weight_perm(zs, 1))  16.3 us
    all_to_all x1, starting transfers between devices, body(): tok = lax.all_to_all(tok, ('x', 'y'), 0, 0)  9.26 us
    ppermute x2, starting transfers between devices, body(): got = lax.ppermute(send, 'core', core_swap)  7.38 us
    ppermute x1, starting transfers between devices, body(): far = lax.ppermute(far, yc, pair_swap(1))  5.3 us
    ppermute x1, starting transfers between devices, body(): flip = lax.ppermute(flip, zyc, weight_perm(zs, 1))  4.84 us
    all_to_all x1, starting transfers between devices, body(): got = lax.all_to_all(pay, ('z', 'core'), 0, 0, axis_index_groups=groups)  3.8 us
  transfers between devices with their start and end apart: 10, of which 6 were waited for; matrix products, arithmetic and copies ran while one was open for 0% of the time, Pallas kernels for 4%

profile of v3, /device:TPU:7, one launch (start us, length us, event | category | flops | bytes accessed | tf_op | source)
XLA Modules:
  0.0 140.1 jit_solution(14070978450448613475)
XLA Ops:
  0.0 0.0 copy-start
  0.0 0.9 copy-done
  0.9 0.1 shard_map.37
  1.0 2.6 %collective-permute-start = (bf16[256,128]{1,0:T(8,128)(2,1)S(1)}, bf16[256,128]{1,0:T(8,128)(2,1)S(1)}, u32[]{:S(2)}, u32[]{:S(2)}) collective-permute-start(bf16[256,128]{1,0:T(8,128)(2,1)S(1)} %get-tuple-element.22), channel_id=1, source_target_pairs={{0,1},{1,0},{2,3},{3,2},{4,5},{5,4},{6,7},{7,6},{8,9},{9,8},{10,11... | collective-permute-start | bytes 196616 | tf_op jit(solution)/shard_map/ppermute | solution.py:317
  3.6 0.9 collective-permute-done
  4.5 1.8 %broadcast_in_dim.2 = bf16[16,2,256,128]{3,2,1,0:T(8,128)(2,1)} broadcast(bf16[2,256,128]{2,1,0:T(8,128)(2,1)S(1)} %pad_maximum_fusion), dimensions={1,2,3} | broadcast | bytes 2228224 | tf_op jit(solution)/shard_map/broadcast_in_dim | solution.py:319
  6.3 0.0 copy-start.2
  6.3 9.3 %all-to-all-start = ((bf16[16,2,256,128]{3,2,1,0:T(8,128)(2,1)}), bf16[16,2,256,128]{3,2,1,0:T(8,128)(2,1)S(1)}, u32[]{:S(2)}, u32[]{:S(2)}) async-start(bf16[16,2,256,128]{3,2,1,0:T(8,128)(2,1)} %broadcast_in_dim.2), calls=%async_computation | async-start | bytes 4194304 | tf_op jit(solution)/shard_map/all_to_all | solution.py:320
  15.6 0.0 copy-done.2
  15.6 4.8 %collective-permute-start.2 = (bf16[3,32,128]{2,1,0:T(8,128)(2,1)S(1)}, bf16[3,32,128]{2,1,0:T(8,128)(2,1)S(1)}, u32[]{:S(2)}, u32[]{:S(2)}) collective-permute-start(bf16[3,32,128]{2,1,0:T(8,128)(2,1)S(1)} %get-tuple-element.40), channel_id=1, source_target_pairs={{0,8},{1,24},{8,0},{9,16},{16,9},{17,25},{24,1},{25,17},{32,41},{3... | collective-permute-start | bytes 73736 | tf_op jit(solution)/shard_map/ppermute | solution.py:314
  20.4 2.2 %collective-permute-start.1 = (bf16[3,32,128]{2,1,0:T(8,128)(2,1)S(1)}, bf16[3,32,128]{2,1,0:T(8,128)(2,1)S(1)}, u32[]{:S(2)}, u32[]{:S(2)}) collective-permute-start(bf16[3,32,128]{2,1,0:T(8,128)(2,1)S(1)} %get-tuple-element.39), channel_id=1, source_target_pairs={{0,0},{1,16},{8,8},{9,24},{16,1},{17,17},{24,9},{25,25},{32,33},{3... | collective-permute-start | bytes 73736 | tf_op jit(solution)/shard_map/ppermute | solution.py:313
  22.7 16.3 %collective-permute-done.2 = bf16[3,32,128]{2,1,0:T(8,128)(2,1)S(1)} collective-permute-done((bf16[3,32,128]{2,1,0:T(8,128)(2,1)S(1)}, bf16[3,32,128]{2,1,0:T(8,128)(2,1)S(1)}, u32[]{:S(2)}, u32[]{:S(2)}) %collective-permute-start.2) | collective-permute-done | bytes 24608 | tf_op jit(solution)/shard_map/ppermute | solution.py:314
  39.0 1.1 collective-permute-done.1
  40.1 35.1 %all-gather = bf16[32,3,32,128]{3,2,1,0:T(8,128)(2,1)S(1)} all-gather(bf16[2,3,32,128]{3,2,1,0:T(8,128)(2,1)S(1)} %pad_maximum_fusion.2), channel_id=2, replica_groups={{0,33,64,97,128,161,192,225,256,289,320,353,384,417,448,481},{1,32,65,9..., dimensions={0}, use_global_device_ids=true | all-gather | bytes 835584 | tf_op jit(solution)/shard_map/all_gather | solution.py:321
  75.2 0.0 all-to-all-done.tok
  75.2 0.8 shard_map.39
  76.0 4.8 %collective-permute-start.3 = (f32[512,384]{1,0:T(8,128)S(1)}, f32[512,384]{1,0:T(8,128)S(1)}, u32[]{:S(2)}, u32[]{:S(2)}) collective-permute-start(f32[512,384]{1,0:T(8,128)S(1)} %shard_map.39), channel_id=1, source_target_pairs={{0,1},{1,0},{2,3},{3,2},{4,5},{5,4},{6,7},{7,6},{8,9},{9,8},{10,11... | collective-permute-start | bytes 2359304 | tf_op jit(solution)/shard_map/ppermute | solution.py:326
  80.8 0.8 shard_map.38.keep
  81.7 0.0 copy-start.1
  81.7 1.0 collective-permute-done.3.got
  82.7 2.3 %shard_map.40 = (f32[512,128]{1,0:T(8,128)S(1)}, f32[512,128]{1,0:T(8,128)S(1)}, f32[512,128]{1,0:T(8,128)S(1)}, f32[3,128,128]{2,1,0:T(8,128)S(1)}, f32[4,200,128]{2,1,0:T(8,128)}) custom-call(f32[512,384]{1,0:T(8,128)S(1)} %shard_map.38.keep, f32[512,384]{1,0:T(8,128)S(1)} %collective-permute-done.3.got), custom_call_target="tpu_custom_call" | custom-call | flops 600000000 | bytes 3000000 | tf_op jit(solution)/shard_map/pallas_call | solution.py:328
  85.0 3.8 %all-to-all-start.1 = ((f32[4,200,128]{2,1,0:T(8,128)}), f32[4,200,128]{2,1,0:T(8,128)S(1)}, u32[]{:S(2)}, u32[]{:S(2)}) async-start(f32[4,200,128]{2,1,0:T(8,128)} %get-tuple-element.27), calls=%async_computation.1 | async-start | bytes 819200 | tf_op jit(solution)/shard_map/all_to_all | solution.py:335
  88.8 0.0 copy-done.1
  88.8 2.0 %collective-permute-start.5 = (f32[2,128]{1,0:T(2,128)S(1)}, f32[2,128]{1,0:T(2,128)S(1)}, u32[]{:S(2)}, u32[]{:S(2)}) collective-permute-start(f32[2,128]{1,0:T(2,128)S(1)} %bitcast.15), channel_id=1, source_target_pairs={{0,1},{1,0},{2,3},{3,2},{4,5},{5,4},{6,7},{7,6},{8,9},{9,8},{10,11... | collective-permute-start | bytes 3080 | tf_op jit(solution)/shard_map/ppermute | solution.py:338
  90.8 1.5 %shard_map.41.raw_ref = f32[512,128]{1,0:T(8,128)S(1)} custom-call(f32[512,128]{1,0:T(8,128)S(1)} %get-tuple-element.23.q_ref, f32[512,128]{1,0:T(8,128)S(1)} %get-tuple-element.25.k_ref, f32[512,128]{1,0:T(8,128)S(1)} %get-tuple-element.24.v_ref, f32[3,128,128]{2,1,0:T(8,128)S(1)} %get-tuple-element.26.blk_ref), custom_call_target="tpu_custom_call" | custom-call | flops 800000000 | bytes 2000000 | tf_op jit(solution)/shard_map/pallas_call | solution.py:339
  92.3 3.1 %all-to-all-done.1.got = f32[4,200,128]{2,1,0:T(8,128)S(1)} async-done(((f32[4,200,128]{2,1,0:T(8,128)}), f32[4,200,128]{2,1,0:T(8,128)S(1)}, u32[]{:S(2)}, u32[]{:S(2)}) %all-to-all-start.1) | async-done | bytes 409632 | tf_op jit(solution)/shard_map/all_to_all | solution.py:335
  95.5 0.5 shard_map.42
  96.0 29.5 %all-gather.1 = f32[1664,128]{1,0:T(8,128)S(1)} all-gather(f32[104,128]{1,0:T(8,128)S(1)} %get-tuple-element.28), channel_id=3, replica_groups={{0,33,64,97,128,161,192,225,256,289,320,353,384,417,448,481},{1,32,65,9..., dimensions={0}, use_global_device_ids=true | all-gather | bytes 905216 | tf_op jit(solution)/shard_map/all_gather | solution.py:347
  125.4 1.0 shard_map.43
  126.4 2.0 %collective-permute-start.4 = (f32[128,64]{1,0:T(8,128)S(1)}, f32[128,64]{1,0:T(8,128)S(1)}, u32[]{:S(2)}, u32[]{:S(2)}) collective-permute-start(f32[128,64]{1,0:T(8,128)S(1)} %get-tuple-element.33), channel_id=1, source_target_pairs={{0,1},{1,0},{2,3},{3,2},{4,5},{5,4},{6,7},{7,6},{8,9},{9,8},{10,11... | collective-permute-start | bytes 98312 | tf_op jit(solution)/shard_map/ppermute | solution.py:352
  128.4 1.1 shard_map.44.raw_ref
  129.5 0.0 collective-permute-done.5.gain_far_ref
  129.6 0.0 collective-permute-done.4.other_ref
  129.6 0.7 shard_map.45
  130.3 1.9 %collective-permute-start.6 = (bf16[256,128]{1,0:T(8,128)(2,1)S(1)}, bf16[256,128]{1,0:T(8,128)(2,1)S(1)}, u32[]{:S(2)}, u32[]{:S(2)}) collective-permute-start(bf16[256,128]{1,0:T(8,128)(2,1)S(1)} %get-tuple-element.35), channel_id=1, source_target_pairs={{0,0},{1,16},{8,8},{9,24},{16,1},{17,17},{24,9},{25,25},{2,2},{3,1... | collective-permute-start | bytes 196616 | tf_op jit(solution)/shard_map/ppermute | solution.py:356
  132.2 5.3 %collective-permute-start.7 = (bf16[256,128]{1,0:T(8,128)(2,1)S(1)}, bf16[256,128]{1,0:T(8,128)(2,1)S(1)}, u32[]{:S(2)}, u32[]{:S(2)}) collective-permute-start(bf16[256,128]{1,0:T(8,128)(2,1)S(1)} %get-tuple-element.36), channel_id=1, source_target_pairs={{0,8},{1,24},{8,0},{9,16},{16,9},{17,25},{24,1},{25,17},{2,10},{3,... | collective-permute-start | bytes 196616 | tf_op jit(solution)/shard_map/ppermute | solution.py:357
  137.5 0.0 collective-permute-done.6
  137.5 1.9 %collective-permute-done.7 = bf16[256,128]{1,0:T(8,128)(2,1)S(1)} collective-permute-done((bf16[256,128]{1,0:T(8,128)(2,1)S(1)}, bf16[256,128]{1,0:T(8,128)(2,1)S(1)}, u32[]{:S(2)}, u32[]{:S(2)}) %collective-permute-start.7) | collective-permute-done | bytes 65568 | tf_op jit(solution)/shard_map/ppermute | solution.py:357
  139.5 0.7 pad_maximum_fusion.1
  (4 shorter events, 0.0 us)
Async XLA Ops:
  0.0 0.9 copy-start
  1.0 3.5 %collective-permute-start = (bf16[256,128]{1,0:T(8,128)(2,1)S(1)}, bf16[256,128]{1,0:T(8,128)(2,1)S(1)}, u32[]{:S(2)}, u32[]{:S(2)}) collective-permute-start(bf16[256,128]{1,0:T(8,128)(2,1)S(1)} %get-tuple-element.22), channel_id=1, source_target_pairs={{0,1},{1,0},{2,3},{3,2},{4,5},{5,4},{6,7},{7,6},{8,9},{9,8},{10,11... | collective-permute-start | bytes 196616 | tf_op jit(solution)/shard_map/ppermute | solution.py:317
  6.3 9.3 %copy-start.2 = (bf16[32,3,256]{2,0,1:T(8,128)(2,1)S(1)}, bf16[32,3,256]{2,0,1:T(8,128)(2,1)}, u32[]{:S(2)}) copy-start(bf16[32,3,256]{2,0,1:T(8,128)(2,1)} %param.4) | copy-start | bytes 147460
  6.3 68.9 %all-to-all-start = ((bf16[16,2,256,128]{3,2,1,0:T(8,128)(2,1)}), bf16[16,2,256,128]{3,2,1,0:T(8,128)(2,1)S(1)}, u32[]{:S(2)}, u32[]{:S(2)}) async-start(bf16[16,2,256,128]{3,2,1,0:T(8,128)(2,1)} %broadcast_in_dim.2), calls=%async_computation | async-start | bytes 4194304 | tf_op jit(solution)/shard_map/all_to_all | solution.py:320
  15.6 23.4 %collective-permute-start.2 = (bf16[3,32,128]{2,1,0:T(8,128)(2,1)S(1)}, bf16[3,32,128]{2,1,0:T(8,128)(2,1)S(1)}, u32[]{:S(2)}, u32[]{:S(2)}) collective-permute-start(bf16[3,32,128]{2,1,0:T(8,128)(2,1)S(1)} %get-tuple-element.40), channel_id=1, source_target_pairs={{0,8},{1,24},{8,0},{9,16},{16,9},{17,25},{24,1},{25,17},{32,41},{3... | collective-permute-start | bytes 73736 | tf_op jit(solution)/shard_map/ppermute | solution.py:314
  20.4 19.6 %collective-permute-start.1 = (bf16[3,32,128]{2,1,0:T(8,128)(2,1)S(1)}, bf16[3,32,128]{2,1,0:T(8,128)(2,1)S(1)}, u32[]{:S(2)}, u32[]{:S(2)}) collective-permute-start(bf16[3,32,128]{2,1,0:T(8,128)(2,1)S(1)} %get-tuple-element.39), channel_id=1, source_target_pairs={{0,0},{1,16},{8,8},{9,24},{16,1},{17,17},{24,9},{25,25},{32,33},{3... | collective-permute-start | bytes 73736 | tf_op jit(solution)/shard_map/ppermute | solution.py:313
  76.0 6.7 %collective-permute-start.3 = (f32[512,384]{1,0:T(8,128)S(1)}, f32[512,384]{1,0:T(8,128)S(1)}, u32[]{:S(2)}, u32[]{:S(2)}) collective-permute-start(f32[512,384]{1,0:T(8,128)S(1)} %shard_map.39), channel_id=1, source_target_pairs={{0,1},{1,0},{2,3},{3,2},{4,5},{5,4},{6,7},{7,6},{8,9},{9,8},{10,11... | collective-permute-start | bytes 2359304 | tf_op jit(solution)/shard_map/ppermute | solution.py:326
  81.7 7.1 %copy-start.1 = (f32[256]{0:T(256)S(1)}, f32[256]{0:T(256)}, u32[]{:S(2)}) copy-start(f32[256]{0:T(256)} %param.5) | copy-start | bytes 3076
  85.0 10.4 %all-to-all-start.1 = ((f32[4,200,128]{2,1,0:T(8,128)}), f32[4,200,128]{2,1,0:T(8,128)S(1)}, u32[]{:S(2)}, u32[]{:S(2)}) async-start(f32[4,200,128]{2,1,0:T(8,128)} %get-tuple-element.27), calls=%async_computation.1 | async-start | bytes 819200 | tf_op jit(solution)/shard_map/all_to_all | solution.py:335
  88.8 40.7 %collective-permute-start.5 = (f32[2,128]{1,0:T(2,128)S(1)}, f32[2,128]{1,0:T(2,128)S(1)}, u32[]{:S(2)}, u32[]{:S(2)}) collective-permute-start(f32[2,128]{1,0:T(2,128)S(1)} %bitcast.15), channel_id=1, source_target_pairs={{0,1},{1,0},{2,3},{3,2},{4,5},{5,4},{6,7},{7,6},{8,9},{9,8},{10,11... | collective-permute-start | bytes 3080 | tf_op jit(solution)/shard_map/ppermute | solution.py:338
  126.4 3.1 %collective-permute-start.4 = (f32[128,64]{1,0:T(8,128)S(1)}, f32[128,64]{1,0:T(8,128)S(1)}, u32[]{:S(2)}, u32[]{:S(2)}) collective-permute-start(f32[128,64]{1,0:T(8,128)S(1)} %get-tuple-element.33), channel_id=1, source_target_pairs={{0,1},{1,0},{2,3},{3,2},{4,5},{5,4},{6,7},{7,6},{8,9},{9,8},{10,11... | collective-permute-start | bytes 98312 | tf_op jit(solution)/shard_map/ppermute | solution.py:352
  130.3 7.2 %collective-permute-start.6 = (bf16[256,128]{1,0:T(8,128)(2,1)S(1)}, bf16[256,128]{1,0:T(8,128)(2,1)S(1)}, u32[]{:S(2)}, u32[]{:S(2)}) collective-permute-start(bf16[256,128]{1,0:T(8,128)(2,1)S(1)} %get-tuple-element.35), channel_id=1, source_target_pairs={{0,0},{1,16},{8,8},{9,24},{16,1},{17,17},{24,9},{25,25},{2,2},{3,1... | collective-permute-start | bytes 196616 | tf_op jit(solution)/shard_map/ppermute | solution.py:356
  132.2 7.2 %collective-permute-start.7 = (bf16[256,128]{1,0:T(8,128)(2,1)S(1)}, bf16[256,128]{1,0:T(8,128)(2,1)S(1)}, u32[]{:S(2)}, u32[]{:S(2)}) collective-permute-start(bf16[256,128]{1,0:T(8,128)(2,1)S(1)} %get-tuple-element.36), channel_id=1, source_target_pairs={{0,8},{1,24},{8,0},{9,16},{16,9},{17,25},{24,1},{25,17},{2,10},{3,... | collective-permute-start | bytes 196616 | tf_op jit(solution)/shard_map/ppermute | solution.py:357
